TPU v7x, 512 devices: a whole 4x4x16 slice. The times are simulated.
512 devices in a mesh: pts: 64 (over x, z), cand: 8 (over y, core).
Axes of the slice: x: 4, y: 4, z: 16, core: 2. Of those that a mesh axis runs over, the one named last changes fastest.
Arguments:
- points: bfloat16 [32768, 4096], P('pts'), may hold values from -6 to 6
- weights: float32 [32768], P('pts'), may hold values from 0.25 to 4
- coverage: float32 [32768], P('pts'), may hold values from 0 to 1.5
- cand_index: int32 [2, 4096], P(None, 'pts'), may hold values from 0 to 511
- winners: int32 [2], replicated, may hold values from 0 to 4095
Outputs:
- gains: float32 [2, 4096], P(None, ('pts', 'cand'))
- final_cover: float32 [32768], P('pts')
All inputs are finite; a program needn't handle non-finite values.
Results may differ from a plain program's by a relative error of at most 0.0003.
Values may be sent and summed in bfloat16 or wider, within the bound.
No kernel may reach another device: no remote copies, remote signals or barrier semaphores. Data moves between devices by JAX's collectives and lax.ppermute only.
A program may use at most 64 MiB of HBM per device.

v0:
```python
import jax
import jax.numpy as jnp
from jax import lax
from jax.sharding import Mesh
from jax.sharding import PartitionSpec as P

PTS = ("pts_0", "pts_1")
PTS_CAND = ("pts_0", "pts_1", "cand")


def joined_along(blocks, dim):
    blocks = jnp.moveaxis(blocks, 0, dim)
    dims = blocks.shape
    return blocks.reshape(*dims[:dim], dims[dim] * dims[dim + 1], *dims[dim + 2 :])


def gather_in_order(array, axes, order):
    blocks = array[None]
    for k in order:
        blocks = lax.all_gather(blocks, axes[k], axis=0, tiled=True)
    block = [lax.axis_size(axes[k]) for k in reversed(order)]
    blocks = blocks.reshape(*block, *array.shape)
    turned = sorted(range(len(order)), key=lambda place: order[len(order) - 1 - place])
    return blocks.transpose(*turned, *range(len(order), blocks.ndim)).reshape(-1, *array.shape)


def whole_of(array, axes, order, dim):
    return joined_along(gather_in_order(array, axes, order), dim)


def from_root(array, axis, root):
    return lax.dynamic_index_in_dim(lax.all_gather(array, axis), root, 0, keepdims=False)


def over_axes(array, axes):
    for axis in axes:
        array = lax.psum(array, axis)
    return array


def gain_terms(points, rows, weights, cover, scale, total):
    sim = (
        lax.dot_general(points, rows, (((1,), (1,)), ((), ())), preferred_element_type=jnp.float32)
        * scale
    )
    return jnp.sum(weights[:, None] * jnp.maximum(sim - cover[:, None], 0.0), axis=0) / total


def body(points, weights, coverage, cand_index, winners):
    rows_dev = points.shape[0]
    width = points.shape[1]
    n_pts = lax.axis_size(PTS)
    n_cand = lax.axis_size("cand")
    per_row = cand_index.shape[1]
    per_dev = per_row // n_cand
    total = float(rows_dev * n_pts)
    scale = width ** (-0.5)
    my_cand = lax.axis_index("cand")
    my_pts = lax.axis_index(PTS)
    mine = lax.dynamic_slice_in_dim(cand_index, my_cand * per_dev, per_dev, 1)
    cover = coverage
    partials = []
    for step in range(cand_index.shape[0]):
        picked = jnp.take(points, mine[step], axis=0)
        frozen = cover
        block = whole_of(picked, PTS, (0, 1), 0)
        part = gain_terms(points, block, weights, frozen, scale, total)
        partials.append(part)
        column = winners[step]
        owner_pts = column // per_row
        owner_cand = column // per_dev % n_cand
        slot = column % per_dev
        local = lax.dynamic_slice_in_dim(block, owner_pts * per_dev + slot, 1, 0)
        chosen = from_root(local, "cand", owner_cand)
        sim = (
            lax.dot_general(
                points, chosen, (((1,), (1,)), ((), ())), preferred_element_type=jnp.float32
            )[:, 0]
            * scale
        )
        cover = jnp.maximum(cover, sim)
    summed = over_axes(jnp.stack(partials), PTS)
    gains = lax.dynamic_slice_in_dim(summed, my_pts * per_dev, per_dev, 1)
    return (gains, cover)


def solution(mesh):
    torus = Mesh(mesh.devices.reshape(4, 16, mesh.shape["cand"]), ("pts_0", "pts_1", "cand"))
    in_specs = (P(PTS, None), P(PTS), P(PTS), P(None, PTS), P())
    out_specs = (P(None, PTS_CAND), P(PTS))
    return jax.shard_map(body, mesh=torus, in_specs=in_specs, out_specs=out_specs, check_vma=False)
```

profile of v0, /device:TPU:24, one launch (start us, length us, event | category | flops | bytes accessed | tf_op | source)
XLA Modules:
  0.0 253.3 jit_solution(13661099396639185572)
XLA Ops:
  7.2 0.0 copy-start
  7.2 0.0 all-gather.9.cloned.1.call-start
  7.2 0.6 copy-done
  7.8 0.1 constant_dynamic-slice_fusion.1
  7.9 3.4 %gather_fusion = bf16[8,4096]{1,0:T(8,128)(2,1)S(1)} fusion(bf16[512,4096]{1,0:T(8,128)(2,1)} %param.7, s32[1024]{0:T(1024)S(1)} %pad_clamp_fusion.1), kind=kCustom, calls=%fused_computation.clone | custom fusion | bytes 131104 | tf_op jit(solution)/shard_map/jit(_take)/gather | solution.py:64
  11.3 0.1 broadcast_select_fusion.1
  11.4 13.3 %all-gather = bf16[32,4096]{1,0:T(8,128)(2,1)} all-gather(bf16[8,4096]{1,0:T(8,128)(2,1)S(1)} %broadcast_select_fusion.1), channel_id=2, replica_groups=mesh['pts_0'=4,'pts_1'=16,'cand'=8] {'pts_0'}, dimensions={0}, use_global_device_ids=true | all-gather | bytes 327680 | tf_op jit(solution)/shard_map/all_gather | solution.py:20
  24.7 0.0 all-gather.9.cloned.1.call-update
  24.8 0.0 all-gather.11.cloned.1.call-start
  24.8 3.4 %gather_fusion.1 = bf16[8,4096]{1,0:T(8,128)(2,1)S(1)} fusion(bf16[512,4096]{1,0:T(8,128)(2,1)} %param.7, s32[1024]{0:T(1024)S(1)} %pad_clamp_fusion), kind=kCustom, calls=%fused_computation.1.clone | custom fusion | bytes 131104 | tf_op jit(solution)/shard_map/jit(_take)/gather | solution.py:64
  28.2 0.1 broadcast_select_fusion
  28.3 13.0 %all-gather.1 = bf16[32,4096]{1,0:T(8,128)(2,1)} all-gather(bf16[8,4096]{1,0:T(8,128)(2,1)S(1)} %broadcast_select_fusion), channel_id=3, replica_groups=mesh['pts_0'=4,'pts_1'=16,'cand'=8] {'pts_0'}, dimensions={0}, use_global_device_ids=true | all-gather | bytes 327680 | tf_op jit(solution)/shard_map/all_gather | solution.py:20
  41.3 0.0 all-gather.11.cloned.1.call-update
  41.3 1.3 fusion.16
  47.9 59.6 %all-gather.9.cloned.1.call-done = bf16[64,8,4096]{2,1,0:T(8,128)(2,1)} async-done(((bf16[4,8,4096]{2,1,0:T(8,128)(2,1)}), bf16[64,8,4096]{2,1,0:T(8,128)(2,1)}) %all-gather.9.cloned.1.call-update) | async-done | bytes 4194320 | tf_op jit(solution)/shard_map/all_gather | solution.py:20
  107.6 2.6 %copy.9 = bf16[4,16,8,4096]{3,2,1,0:T(8,128)(2,1)S(1)} copy(bf16[4,16,8,4096]{3,2,0,1:T(8,128)(2,1)} %bitcast.42) | data formatting | bytes 8388608 | tf_op jit(solution)/shard_map/transpose | solution.py:24
  110.2 12.8 %all-gather.4 = bf16[8,1,4096]{2,1,0:T(2,128)(2,1)S(1)} all-gather(bf16[1,1,4096]{2,1,0:T(2,128)(2,1)S(1)} %dynamic-slice_bitcast_fusion.1), channel_id=4, replica_groups=mesh['pts_0'=4,'pts_1'=16,'cand'=8] {'cand'}, dimensions={0}, use_global_device_ids=true | all-gather | bytes 73728 | tf_op jit(solution)/shard_map/all_gather | solution.py:32
  123.0 0.0 copy-done.1
  123.0 0.0 copy-done.3
  123.0 0.0 copy-done.4
  123.0 2.4 fusion.7
  125.4 59.6 %all-gather.11.cloned.1.call-done = bf16[64,8,4096]{2,1,0:T(8,128)(2,1)} async-done(((bf16[4,8,4096]{2,1,0:T(8,128)(2,1)}), bf16[64,8,4096]{2,1,0:T(8,128)(2,1)}) %all-gather.11.cloned.1.call-update) | async-done | bytes 4194320 | tf_op jit(solution)/shard_map/all_gather | solution.py:20
  184.9 2.6 %copy.10 = bf16[4,16,8,4096]{3,2,1,0:T(8,128)(2,1)S(1)} copy(bf16[4,16,8,4096]{3,2,0,1:T(8,128)(2,1)} %bitcast.43) | data formatting | bytes 8388608 | tf_op jit(solution)/shard_map/transpose | solution.py:24
  187.6 12.8 %all-gather.5 = bf16[8,1,4096]{2,1,0:T(2,128)(2,1)S(1)} all-gather(bf16[1,1,4096]{2,1,0:T(2,128)(2,1)S(1)} %dynamic-slice_bitcast_fusion), channel_id=5, replica_groups=mesh['pts_0'=4,'pts_1'=16,'cand'=8] {'cand'}, dimensions={0}, use_global_device_ids=true | all-gather | bytes 73728 | tf_op jit(solution)/shard_map/all_gather | solution.py:32
  200.3 0.0 copy-done.2
  200.4 1.2 fusion.10
  201.5 1.2 fusion.8
  202.7 0.6 multiply_maximum_fusion
  203.3 2.4 fusion.6
  205.8 10.4 %psum.14 = f32[2,512]{1,0:T(2,128)S(1)} all-reduce(f32[2,512]{1,0:T(2,128)S(1)} %pad_maximum_fusion), channel_id=1, replica_groups=mesh['pts_0'=4,'pts_1'=16,'cand'=8] {'pts_0'}, use_global_device_ids=true, to_apply=%region_2.4 | all-reduce | flops 1024 | bytes 8192 | tf_op jit(solution)/shard_map/psum | solution.py:37
  216.2 29.6 %psum.15 = f32[2,512]{1,0:T(2,128)S(1)} all-reduce(f32[2,512]{1,0:T(2,128)S(1)} %psum.14), channel_id=1, replica_groups=mesh['pts_0'=4,'pts_1'=16,'cand'=8] {'pts_1'}, use_global_device_ids=true, to_apply=%region_3.5 | all-reduce | flops 1024 | bytes 8192 | tf_op jit(solution)/shard_map/psum | solution.py:37
  245.8 0.6 constant_dynamic-slice_fusion
  (12 shorter events, 0.1 us)
Async XLA Ops:
  7.2 0.7 copy-start
  7.2 100.4 %all-gather.9.cloned.1.call-start = ((), (), s32[]{:S(2)}) async-start(), calls=%async_computation | async-start | bytes 4456448 | tf_op jit(solution)/shard_map/all_gather | solution.py:20
  24.8 160.2 %all-gather.11.cloned.1.call-start = ((), (), s32[]{:S(2)}) async-start(), calls=%async_computation.1 | async-start | bytes 4456448 | tf_op jit(solution)/shard_map/all_gather | solution.py:20
  107.6 15.4 %copy-start.1 = (bf16[512,4096]{1,0:T(8,128)(2,1)S(1)}, bf16[512,4096]{1,0:T(8,128)(2,1)}, u32[]{:S(2)}) copy-start(bf16[512,4096]{1,0:T(8,128)(2,1)} %param.7) | copy-start | bytes 12582916
  107.6 15.4 %copy-start.3 = (f32[512]{0:T(512)S(1)}, f32[512]{0:T(512)}, u32[]{:S(2)}) copy-start(f32[512]{0:T(512)} %param.9) | copy-start | bytes 6148
  107.6 15.4 %copy-start.4 = (f32[512]{0:T(512)S(1)}, f32[512]{0:T(512)}, u32[]{:S(2)}) copy-start(f32[512]{0:T(512)} %param.8) | copy-start | bytes 6148
  184.9 15.4 %copy-start.2 = (bf16[512,4096]{1,0:T(8,128)(2,1)S(1)}, bf16[512,4096]{1,0:T(8,128)(2,1)}, u32[]{:S(2)}) copy-start(bf16[512,4096]{1,0:T(8,128)(2,1)} %param.7) | copy-start | bytes 12582916
Sparse Core Ops, SparseCore 0:
  24.9 82.6 all-gather.8
  109.6 75.2 all-gather.10
where the time goes:
time: 254 us; the launch traced here: 253 us
  waiting for transfers between devices  119 us (47%)
  blocking collectives  91.9 us (36%)
  between operations  19.4 us (8%)
  local copies, waits for them, and re-layouts  14.7 us (6%)
  matrix products  7.19 us (3%)
    all_gather x2, waiting for transfers between devices, gather_in_order(): blocks = lax.all_gather(blocks, axes[k], axis=0, tiled=True)  119 us
    psum x2, blocking collectives, over_axes(): array = lax.psum(array, axis)  40 us
    all_gather x2, blocking collectives, gather_in_order(): blocks = lax.all_gather(blocks, axes[k], axis=0, tiled=True)  26.3 us
    all_gather x2, blocking collectives, from_root(): lax.all_gather(array, axis)  25.5 us
    gather x2, local copies, waits for them, and re-layouts, body(): picked = jnp.take(points, mine[step], axis=0)  6.75 us
    transpose x2, local copies, waits for them, and re-layouts, gather_in_order(): blocks.transpose(*turned, *range(len(order), blocks.ndim))  5.22 us
  transfers between devices with their start and end apart: 2, of which 2 were waited for; matrix products, arithmetic and copies ran while one was open for 4% of the time, Pallas kernels for 0%

commit v1 on v0

v1 whole, which is shorter than its diff:
```python
import jax
import jax.numpy as jnp
from jax import lax
from jax.sharding import Mesh
from jax.sharding import PartitionSpec as P

PTS = ("pts_0", "pts_1")
PTS_CAND = ("pts_0", "pts_1", "cand")
LIFT = 2.0**13


def body(points, weights, coverage, cand_index, winners):
    rows_dev, width = points.shape
    steps, per_row = cand_index.shape
    n_x, n_z = (lax.axis_size(axis) for axis in PTS)
    n_cand = lax.axis_size("cand")
    per_dev = per_row // n_cand
    held = steps * per_dev
    total = float(rows_dev * n_x * n_z)
    scale = width ** (-0.5) / LIFT
    my_cand = lax.axis_index("cand")
    my_pts = lax.axis_index(PTS)

    mine = lax.dynamic_slice_in_dim(cand_index, my_cand * per_dev, per_dev, 1).reshape(-1)
    owner = winners // per_row
    won = jnp.take_along_axis(cand_index, (winners % per_row)[:, None], axis=1)[:, 0]
    won = jnp.where(owner == my_pts, won, -1)
    wanted = jnp.concatenate([mine, won])
    pick = jnp.where(
        wanted[:, None] == lax.broadcasted_iota(jnp.int32, (held + steps, rows_dev), 1), LIFT, 0.0
    ).astype(points.dtype)
    picked = lax.dot_general(
        pick, points, (((1,), (0,)), ((), ())), preferred_element_type=jnp.float32
    ).astype(jnp.float16)
    piece = steps * width // held
    sent = jnp.concatenate([picked[:held], picked[held:].reshape(held, piece)], axis=1)

    along_z = lax.all_gather(sent, PTS[1], axis=0, tiled=True)
    owner_x, owner_z = owner // n_z, owner % n_z
    part = held // steps
    chosen = [
        lax.dynamic_slice(along_z, (owner_z[t] * held + t * part, width), (part, piece)).reshape(1, width)
        for t in range(steps)
    ]
    pad = jnp.zeros((8 - steps, width), jnp.float16)
    column = jnp.concatenate([along_z[:, :width], *chosen, pad], axis=0)
    column_rows = n_z * held + 8
    block = lax.all_gather(column, PTS[0], axis=0, tiled=True).astype(points.dtype)
    block = block.reshape(n_x, column_rows, width)
    chosen = jnp.concatenate(
        [
            lax.dynamic_slice(block, (owner_x[t], n_z * held + t, 0), (1, 1, width))[0]
            for t in range(steps)
        ]
    )

    near = (
        lax.dot_general(points, chosen, (((1,), (1,)), ((), ())), preferred_element_type=jnp.float32)
        * scale
    )
    covers = [coverage]
    for t in range(steps):
        covers.append(jnp.maximum(covers[-1], near[:, t]))
    step_of = lax.broadcasted_iota(jnp.int32, (1, 1, n_z * held), 2) % held // per_dev
    cover = covers[0][:, None, None]
    for t in range(1, steps):
        cover = jnp.where(step_of >= t, covers[t][:, None, None], cover)
    sim = (
        lax.dot_general(
            points,
            block[:, : n_z * held],
            (((1,), (2,)), ((), ())),
            preferred_element_type=jnp.float32,
        )
        * scale
    )
    part = jnp.sum(weights[:, None, None] * jnp.maximum(sim - cover, 0.0), axis=0)
    part = lax.all_to_all(part.reshape(n_x * n_z, held), PTS, 0, 0, tiled=True)
    gains = jnp.sum(part, axis=0) / total
    return gains.reshape(steps, per_dev), covers[-1]


def solution(mesh):
    torus = Mesh(mesh.devices.reshape(4, 16, mesh.shape["cand"]), ("pts_0", "pts_1", "cand"))
    in_specs = (P(PTS, None), P(PTS), P(PTS), P(None, PTS), P())
    out_specs = (P(None, PTS_CAND), P(PTS))
    return jax.shard_map(body, mesh=torus, in_specs=in_specs, out_specs=out_specs, check_vma=False)
```

time: 254 us -> 184 us (0.72)
  waiting for transfers between devices: 119 us -> 0 us
  blocking collectives: 91.9 us -> 144 us
  between operations: 19.4 us -> 5.85 us
  other arithmetic: 0.8 us -> 14 us
  local copies, waits for them, and re-layouts: 14.7 us -> 5.64 us
  matrix products: 7.19 us -> 14.5 us
    all_gather x2 -> x0, waiting for transfers between devices: 119 us -> none  [gather_in_order(): blocks = lax.all_gather(blocks, axes[k], axis=0, tiled=True)]
    all_gather x4 -> x2, blocking collectives: 51.8 us -> 120 us  [the longest x1 68.2 us: body(): lax.all_gather(column, PTS[0], axis=0, tiled=True).astype(points.dtype)]
    psum x2 -> x0, blocking collectives: 40 us -> none  [over_axes(): array = lax.psum(array, axis)]
    all_to_all x0 -> x1, blocking collectives: none -> 23.6 us  [body(): part = lax.all_to_all(part.reshape(n_x * n_z, held), PTS, 0, 0, tiled=True)]
    convert_element_type x0 -> x1, other arithmetic: none -> 9.84 us  [body(): lax.all_gather(column, PTS[0], axis=0, tiled=True).astype(points.dtype)]
    dot_general x2, matrix products: 4.82 us -> 11 us  [the longest x1 8.08 us: body(): lax.dot_general(points, block[:, :n_z * held], (((1,), (2,)), ((), ())),...]
    gather x2, local copies, waits for them, and re-layouts: 6.75 us -> 0.74 us  [body(): jnp.take_along_axis(cand_index, (winners % per_row)[:, None], axis=1)[:, 0]]
    transpose x2 -> x0, local copies, waits for them, and re-layouts: 5.22 us -> none  [gather_in_order(): blocks.transpose(*turned, *range(len(order), blocks.ndim))]
  transfers between devices with their start and end apart: 2 -> 0, of which waited for: 2 -> 0; matrix products, arithmetic and copies ran while one was open for 4% -> 0% of each run, Pallas kernels for 0% -> 0%
where the time goes in v1:
time: 184 us
  blocking collectives  144 us (78%)
  matrix products  14.5 us (8%)
  other arithmetic  14 us (8%)
  between operations  5.85 us (3%)
  local copies, waits for them, and re-layouts  5.64 us (3%)
    all_gather x1, blocking collectives, body(): lax.all_gather(column, PTS[0], axis=0, tiled=True).astype(points.dtype)  68.2 us
    all_gather x1, blocking collectives, body(): along_z = lax.all_gather(sent, PTS[1], axis=0, tiled=True)  51.8 us
    all_to_all x1, blocking collectives, body(): part = lax.all_to_all(part.reshape(n_x * n_z, held), PTS, 0, 0, tiled=True)  23.6 us
    convert_element_type x1, other arithmetic, body(): lax.all_gather(column, PTS[0], axis=0, tiled=True).astype(points.dtype)  9.84 us
    dot_general x1, matrix products, body(): lax.dot_general(points, block[:, :n_z * held], (((1,), (2,)), ((), ())),...  8.08 us

profile of v1, /device:TPU:24, one launch (start us, length us, event | category | flops | bytes accessed | tf_op | source)
XLA Modules:
  0.0 183.7 jit_solution(2298904888433843876)
XLA Ops:
  0.6 0.0 copy-start
  0.7 0.7 and_select_fusion
  1.4 0.1 copy.9
  1.4 0.2 or_reduce_fusion
  1.6 0.0 copy-done
  1.6 0.6 gather_fusion
  2.3 0.1 constant_dynamic-slice_fusion
  2.4 0.1 reshape.151
  2.4 0.1 pad_add_fusion.1
  2.5 2.9 %convolution_convert_fusion = f16[18,4096]{1,0:T(8,128)(2,1)S(1)} fusion(bf16[512,4096]{1,0:T(8,128)(2,1)} %param.5, s32[18]{0:T(128)S(1)} %pad_add_fusion.1), kind=kOutput, calls=%fused_computation.3 | convolution fusion | flops 75598848 | bytes 4341832 | tf_op jit(solution)/shard_map/dot_general | solution.py:32
  5.5 0.6 fusion.23
  8.6 51.8 %all-gather.2 = f16[256,4608]{1,0:T(8,128)(2,1)S(1)} all-gather(f16[16,4608]{1,0:T(8,128)(2,1)S(1)} %pad_maximum_fusion), channel_id=1, replica_groups=mesh['pts_0'=4,'pts_1'=16,'cand'=8] {'pts_1'}, dimensions={0}, use_global_device_ids=true | all-gather | bytes 2506752 | tf_op jit(solution)/shard_map/all_gather | solution.py:38
  60.5 0.6 fusion.24
  62.3 1.7 slice.44
  64.1 0.1 pad.5.clone
  64.2 2.4 %maximum_maximum_fusion = f16[264,4096]{1,0:T(8,128)(2,1)S(1)} fusion(f16[1,4096]{1,0:T(2,128)(2,1)S(1)} %bitcast.44, f16[1,4096]{1,0:T(2,128)(2,1)S(1)} %bitcast.43, f16[256,4096]{1,0:T(8,128)(2,1)} %slice.44, f16[264]{0:T(512)(128)(2,1)S(1)} %pad.5.clone), kind=kLoop, calls=%fused_computation.5 | loop fusion | flops 3244032 | bytes 4276752 | tf_op jit(solution)/shard_map/concatenate | solution.py:46
  66.6 68.2 %all-gather.3 = f16[1056,4096]{1,0:T(8,128)(2,1)} all-gather(f16[264,4096]{1,0:T(8,128)(2,1)S(1)} %maximum_maximum_fusion), channel_id=1, replica_groups=mesh['pts_0'=4,'pts_1'=16,'cand'=8] {'pts_0'}, dimensions={0}, use_global_device_ids=true | all-gather | bytes 10813440 | tf_op jit(solution)/shard_map/all_gather | solution.py:48
  134.9 9.8 %convert_element_type.11 = bf16[1056,4096]{1,0:T(8,128)(2,1)} convert(f16[1056,4096]{1,0:T(8,128)(2,1)} %all-gather.3) | non-fusion elementwise | flops 4325376 | bytes 17301504 | tf_op jit(solution)/shard_map/convert_element_type | solution.py:48
  146.0 0.9 dynamic-slice_bitcast_fusion.1
  146.9 0.0 copy-start.1
  146.9 0.0 copy-start.3
  146.9 3.5 %fusion.10 = f32[512,2]{0,1:T(2,128)S(1)} fusion(bf16[512,4096]{1,0:T(8,128)(2,1)} %param.5, bf16[1,4096]{1,0:T(2,128)(2,1)S(1)} %get-tuple-element.7, bf16[1,4096]{1,0:T(2,128)(2,1)S(1)} %get-tuple-element.6), kind=kOutput, calls=%fused_computation.11 | convolution fusion | flops 8422400 | bytes 4214784 | tf_op jit(solution)/shard_map/dot_general | solution.py:58
  150.4 0.0 copy-done.2
  150.5 0.6 fusion.21
  151.0 0.1 broadcast_select_fusion
  151.1 0.0 copy-done.1
  151.2 0.0 copy-done.3
  151.2 8.1 %fusion.5 = f32[4,256]{1,0:T(4,128)S(1)} fusion(bf16[512,4096]{1,0:T(8,128)(2,1)S(1)} %copy-done.1, bf16[4,264,4096]{2,1,0:T(8,128)(2,1)} %bitcast.41, f32[512,256]{0,1:T(8,128)S(1)} %broadcast_select_fusion, f32[512]{0:T(512)S(1)} %copy-done.3), kind=kOutput, calls=%fused_computation.9 | convolution fusion | flops 4297587712 | bytes 13113344 | tf_op jit(solution)/shard_map/dot_general | solution.py:69
  159.3 0.1 all_to_all.6
  159.3 23.6 %all_to_all.9 = f32[64,1,16]{2,1,0:T(1,128)S(1)} all-to-all(f32[64,1,16]{2,1,0:T(1,128)S(1)} %bitcast.42), channel_id=1, replica_groups=mesh['pts_0'=4,'pts_1'=16,'cand'=8] {'pts_0','pts_1'}, dimensions={0} | all-to-all | bytes 8192 | tf_op jit(solution)/shard_map/all_to_all | solution.py:78
  183.0 0.1 reduce_sum.19
  183.1 0.6 div.52
  (15 shorter events, 0.2 us)
Async XLA Ops:
  0.6 1.0 copy-start
  144.7 5.7 %copy-start.2 = (f32[512]{0:T(512)S(1)}, f32[512]{0:T(512)}, u32[]{:S(2)}) copy-start(f32[512]{0:T(512)} %param.7) | copy-start | bytes 6148
  146.9 4.3 %copy-start.1 = (bf16[512,4096]{1,0:T(8,128)(2,1)S(1)}, bf16[512,4096]{1,0:T(8,128)(2,1)}, u32[]{:S(2)}) copy-start(bf16[512,4096]{1,0:T(8,128)(2,1)} %param.5) | copy-start | bytes 12582916
  146.9 4.3 %copy-start.3 = (f32[512]{0:T(512)S(1)}, f32[512]{0:T(512)}, u32[]{:S(2)}) copy-start(f32[512]{0:T(512)} %param.6) | copy-start | bytes 6148

commit v2 on v1

v2 whole, which is shorter than its diff:
```python
import jax
import jax.numpy as jnp
from jax import lax
from jax.sharding import Mesh
from jax.sharding import PartitionSpec as P

PTS = ("pts_0", "pts_1")
PTS_CAND = ("pts_0", "pts_1", "cand")
WIRE = jnp.float16
LIFT = 2.0**13


def dot(a, b):
    return lax.dot_general(a, b, (((1,), (1,)), ((), ())), preferred_element_type=jnp.float32)


def body(points, weights, coverage, cand_index, winners):
    rows_dev, width = points.shape
    steps, per_row = cand_index.shape
    n_x, n_z = (lax.axis_size(axis) for axis in PTS)
    n_cand = lax.axis_size("cand")
    per_dev = per_row // n_cand
    total = float(rows_dev * n_x * n_z)
    scale = width ** (-0.5) / LIFT
    my_cand = lax.axis_index("cand")
    my_step = lax.axis_index(PTS[0]) % steps
    my_core = my_cand % 2
    half = rows_dev // 2

    beside = [(x, x ^ 1) for x in range(n_x)]
    twin = [(c, c ^ 1) for c in range(n_cand)]
    there = lax.ppermute(jnp.stack([weights, coverage]), PTS[0], beside)
    near_half = lax.ppermute(
        lax.dynamic_slice_in_dim(points, my_core * half, half, 0), PTS[0], beside
    )
    far_half = lax.ppermute(near_half, "cand", twin)

    mine = lax.dynamic_slice_in_dim(cand_index, my_cand * per_dev, per_dev, 1).reshape(-1)
    owner = winners // per_row
    won = jnp.take_along_axis(cand_index, (winners % per_row)[:, None], axis=1)[:, 0]
    won = jnp.where(owner == lax.axis_index(PTS), won, -1)
    wanted = jnp.concatenate([mine, won])
    held = steps * per_dev
    pick = jnp.where(
        wanted[:, None] == lax.broadcasted_iota(jnp.int32, (held + steps, rows_dev), 1), LIFT, 0.0
    ).astype(points.dtype)
    picked = lax.dot_general(
        pick, points, (((1,), (0,)), ((), ())), preferred_element_type=jnp.float32
    ).astype(WIRE)
    owner_x, owner_z = owner // n_z, owner % n_z

    piece = steps * width // per_dev
    wins = picked[held:].reshape(per_dev, piece)
    sent = [
        jnp.concatenate([picked[t * per_dev : (t + 1) * per_dev], wins], axis=1)
        for t in range(steps)
    ]
    sent = jnp.stack([sent[x % steps] for x in range(n_x)])
    along_x = lax.all_to_all(sent, PTS[0], 0, 0, tiled=True)
    part = per_dev // steps
    slots = n_x * per_dev
    wins = jnp.concatenate(
        [
            lax.dynamic_slice(along_x, (owner_x[t], t * part, width), (1, part, piece)).reshape(
                slots // steps, steps * width // slots
            )
            for t in range(steps)
        ]
    )
    column = jnp.concatenate([along_x[:, :, :width].reshape(slots, width), wins], axis=1)
    along_z = lax.all_gather(column, PTS[1], axis=0, tiled=True)
    along_z, there = lax.optimization_barrier((along_z, there))
    piece = steps * width // slots
    part = slots // steps
    chosen = jnp.concatenate(
        [
            lax.dynamic_slice(
                along_z, (owner_z[t] * slots + t * part, width), (part, piece)
            ).reshape(1, width)
            for t in range(steps)
        ]
    ).astype(points.dtype)
    block = along_z[:, :width].astype(points.dtype)

    covers = [coverage]
    near = dot(points, chosen) * scale
    for t in range(steps):
        covers.append(jnp.maximum(covers[-1], near[:, t]))

    def gain(rows, weight, cover):
        return jnp.sum(
            weight[:, None] * jnp.maximum(dot(rows, block) * scale - cover[:, None], 0.0), axis=0
        )

    def gain_there(rows, core):
        weight = lax.dynamic_slice_in_dim(there[0], core * half, half)
        cover = lax.dynamic_slice_in_dim(there[1], core * half, half)
        later = jnp.maximum(cover, dot(rows, chosen[:1])[:, 0] * scale)
        return gain(rows, weight, jnp.where(my_step == 0, cover, later))

    part = gain(points, weights, jnp.where(my_step == 0, covers[0], covers[1]))
    part = part + gain_there(near_half, my_core) + gain_there(far_half, 1 - my_core)
    part = part.reshape(n_z, n_x, per_dev).transpose(1, 0, 2).reshape(n_x * n_z, per_dev)
    part = lax.all_to_all(part, PTS, 0, 0, tiled=True)
    part = part.reshape(n_x // steps, steps, n_z, per_dev)
    return jnp.sum(part, axis=(0, 2)) / total, covers[-1]


def solution(mesh):
    torus = Mesh(mesh.devices.reshape(4, 16, mesh.shape["cand"]), ("pts_0", "pts_1", "cand"))
    in_specs = (P(PTS, None), P(PTS), P(PTS), P(None, PTS), P())
    out_specs = (P(None, PTS_CAND), P(PTS))
    return jax.shard_map(body, mesh=torus, in_specs=in_specs, out_specs=out_specs, check_vma=False)
```

time: 184 us -> 134 us (0.73)
  blocking collectives: 144 us -> 95.8 us
  starting transfers between devices: 0 us -> 12.1 us
  other arithmetic: 14 us -> 2.58 us
  matrix products: 14.5 us -> 10.4 us
    all_gather x2 -> x1, blocking collectives: 120 us -> 69.9 us  [body(): along_z = lax.all_gather(column, PTS[1], axis=0, tiled=True)]
    convert_element_type x1, other arithmetic: 9.84 us -> 0.05 us  [body(): chosen = jnp.concatenate([lax.dynamic_slice(along_z, (owner_z[t] * slots...]
    ppermute x0 -> x3, starting transfers between devices: none -> 7.76 us  [the longest x1 3.93 us: body(): there = lax.ppermute(jnp.stack([weights, coverage]), PTS[0], beside)]
    all_to_all x0 -> x1, starting transfers between devices: none -> 4.29 us  [body(): along_x = lax.all_to_all(sent, PTS[0], 0, 0, tiled=True)]
    dot_general x2 -> x6, matrix products: 11.6 us -> 7.55 us  [dot(): lax.dot_general(a, b, (((1,), (1,)), ((), ())), preferred_element_type=jn...]
    dynamic_slice x0 -> x3, local copies, waits for them, and re-layouts: none -> 3.2 us  [the longest x1 3.17 us: body(): lax.dynamic_slice_in_dim(points, my_core * half, half, 0)]
    concatenate x2 -> x1, other arithmetic: 2.46 us -> 0.07 us  [body(): jnp.concatenate([along_x[:, :, :width].reshape(slots, width), wins], axis=1)]
    all_to_all x1, blocking collectives: 23.6 us -> 25.8 us  [body(): part = lax.all_to_all(part, PTS, 0, 0, tiled=True)]
  transfers between devices with their start and end apart: 0 -> 4, of which waited for: 0 -> 0; matrix products, arithmetic and copies ran while one was open for 0% -> 8% of each run, Pallas kernels for 0% -> 0%
where the time goes in v2:
time: 134 us
  blocking collectives  95.8 us (71%)
  starting transfers between devices  12.1 us (9%)
  matrix products  10.4 us (8%)
  local copies, waits for them, and re-layouts  6.97 us (5%)
  between operations  6.05 us (5%)
  other arithmetic  2.58 us (2%)
    all_gather x1, blocking collectives, body(): along_z = lax.all_gather(column, PTS[1], axis=0, tiled=True)  69.9 us
    all_to_all x1, blocking collectives, body(): part = lax.all_to_all(part, PTS, 0, 0, tiled=True)  25.8 us
    dot_general x6, matrix products, dot(): lax.dot_general(a, b, (((1,), (1,)), ((), ())), preferred_element_type=jn...  7.55 us
    all_to_all x1, starting transfers between devices, body(): along_x = lax.all_to_all(sent, PTS[0], 0, 0, tiled=True)  4.29 us
    ppermute x1, starting transfers between devices, body(): there = lax.ppermute(jnp.stack([weights, coverage]), PTS[0], beside)  3.93 us
    dynamic_slice x1, local copies, waits for them, and re-layouts, body(): lax.dynamic_slice_in_dim(points, my_core * half, half, 0)  3.17 us
    dot_general x1, matrix products, body(): lax.dot_general(pick, points, (((1,), (0,)), ((), ())), preferred_element...  2.89 us
  transfers between devices with their start and end apart: 4, of which 0 were waited for; matrix products, arithmetic and copies ran while one was open for 8% of the time, Pallas kernels for 0%

profile of v2, /device:TPU:24, one launch (start us, length us, event | category | flops | bytes accessed | tf_op | source)
XLA Modules:
  0.0 133.9 jit_solution(8243033898988971302)
XLA Ops:
  0.6 0.0 copy-start
  0.7 0.6 copy-done
  1.3 0.1 constant_dynamic-slice_fusion.6
  1.4 0.1 reshape.104
  1.5 0.7 and_select_fusion
  2.2 0.1 copy.10
  2.3 0.2 or_reduce_fusion
  2.5 0.6 gather_fusion
  3.1 0.1 pad_add_fusion.1
  3.2 2.9 %convolution_convert_fusion = f16[18,4096]{1,0:T(8,128)(2,1)S(1)} fusion(bf16[512,4096]{1,0:T(8,128)(2,1)} %param.5, s32[18]{0:T(128)S(1)} %pad_add_fusion.1), kind=kOutput, calls=%fused_computation.1 | convolution fusion | flops 75598848 | bytes 4341832 | tf_op jit(solution)/shard_map/dot_general | solution.py:47
  6.2 0.8 pad_maximum_fusion
  7.0 4.3 %all-to-all-start = ((f16[4,8,5120]{2,1,0:T(8,128)(2,1)}), f16[4,8,5120]{2,1,0:T(8,128)(2,1)S(1)}, u32[]{:S(2)}, u32[]{:S(2)}) async-start(f16[4,8,5120]{2,1,0:T(8,128)(2,1)} %pad_maximum_fusion), calls=%async_computation | async-start | bytes 655360 | tf_op jit(solution)/shard_map/all_to_all | solution.py:59
  11.3 3.9 %collective-permute-start = (f32[2,512]{1,0:T(2,128)S(1)}, f32[2,512]{1,0:T(2,128)S(1)}, u32[]{:S(2)}, u32[]{:S(2)}) collective-permute-start(f32[2,512]{1,0:T(2,128)S(1)} %pad_maximum_fusion.3), channel_id=1, source_target_pairs={{0,128},{128,0},{256,384},{384,256},{1,129},{129,1},{257,385},{385... | collective-permute-start | bytes 12296 | tf_op jit(solution)/shard_map/ppermute | solution.py:32
  15.3 3.2 %constant_dynamic-slice_fusion.3 = bf16[256,4096]{1,0:T(8,128)(2,1)} fusion(bf16[512,4096]{1,0:T(8,128)(2,1)} %param.5, s32[]{:T(128)S(6)} %select_n.114), kind=kLoop, calls=%fused_computation.61 | loop fusion | bytes 4194308 | tf_op jit(solution)/shard_map/dynamic_slice | solution.py:34
  18.5 1.9 %collective-permute-start.1 = (bf16[256,4096]{1,0:T(8,128)(2,1)}, bf16[256,4096]{1,0:T(8,128)(2,1)S(1)}, u32[]{:S(2)}, u32[]{:S(2)}) collective-permute-start(bf16[256,4096]{1,0:T(8,128)(2,1)} %constant_dynamic-slice_fusion.3), channel_id=1, source_target_pairs={{0,128},{128,0},{256,384},{384,256},{1,129},{129,1},{257,385},{385... | collective-permute-start | bytes 6291464 | tf_op jit(solution)/shard_map/ppermute | solution.py:33
  20.4 0.6 fusion.68
  23.5 0.6 fusion.67
  26.8 0.0 copy-start.1
  26.9 0.1 maximum_maximum_fusion
  26.9 69.9 %all-gather.1 = f16[512,4352]{1,0:T(8,128)(2,1)S(1)} all-gather(f16[32,4352]{1,0:T(8,128)(2,1)S(1)} %maximum_maximum_fusion), channel_id=1, replica_groups=mesh['pts_0'=4,'pts_1'=16,'cand'=8] {'pts_1'}, dimensions={0}, use_global_device_ids=true | all-gather | bytes 4734976 | tf_op jit(solution)/shard_map/all_gather | solution.py:71
  97.0 1.2 fusion.54
  98.2 1.9 %collective-permute-start.2 = (bf16[256,4096]{1,0:T(8,128)(2,1)S(1)}, bf16[256,4096]{1,0:T(8,128)(2,1)S(1)}, u32[]{:S(2)}, u32[]{:S(2)}) collective-permute-start(bf16[256,4096]{1,0:T(8,128)(2,1)S(1)} %collective-permute-done.1), channel_id=1, source_target_pairs={{0,1},{1,0},{2,3},{3,2},{4,5},{5,4},{6,7},{7,6},{8,9},{9,8},{10,11... | collective-permute-start | bytes 6291464 | tf_op jit(solution)/shard_map/ppermute | solution.py:36
  100.2 0.6 maximum_maximum_fusion.1
  100.8 2.4 %fusion.21 = f32[512]{0:T(512)S(1)} fusion(bf16[512,4096]{1,0:T(8,128)(2,1)S(1)} %copy-done.1, f16[512,4352]{1,0:T(8,128)(2,1)S(1)} %all-gather.1, f32[512]{0:T(512)S(1)} %get-tuple-element.19, f32[512]{0:T(512)S(1)} %copy-done.3), kind=kOutput, calls=%fused_computation.15 | convolution fusion | flops 2150891008 | bytes 8394752 | tf_op jit(solution)/shard_map/dot_general | solution.py:14
  103.2 0.6 fusion.61
  103.8 1.3 %fusion.48 = f32[512]{0:T(512)S(1)} fusion(bf16[256,4096]{1,0:T(8,128)(2,1)S(1)} %collective-permute-done.1, f16[512,4352]{1,0:T(8,128)(2,1)S(1)} %all-gather.1, f32[256]{0:T(256)S(1)} %maximum_select_fusion.2, f32[256]{0:T(256)S(1)} %bitcast.64), kind=kOutput, calls=%fused_computation.24 | convolution fusion | flops 1076493824 | bytes 6295552 | tf_op jit(solution)/shard_map/dot_general | solution.py:14
  105.2 0.6 fusion.60
  105.8 1.3 fusion.51
  107.2 0.1 add.92
  107.3 25.8 %all_to_all.14 = f32[64,1,8]{2,1,0:T(1,128)S(1)} all-to-all(f32[64,1,8]{2,1,0:T(1,128)S(1)} %bitcast.50), channel_id=1, replica_groups=mesh['pts_0'=4,'pts_1'=16,'cand'=8] {'pts_0','pts_1'}, dimensions={0} | all-to-all | bytes 4096 | tf_op jit(solution)/shard_map/all_to_all | solution.py:104
  133.2 0.1 copy.17
  133.2 0.6 copy.14
  (34 shorter events, 0.4 us)
Async XLA Ops:
  0.6 0.7 copy-start
  0.6 10.7 %copy-start.3 = (f32[512]{0:T(512)S(1)}, f32[512]{0:T(512)}, u32[]{:S(2)}) copy-start(f32[512]{0:T(512)} %param.6) | copy-start | bytes 6148
  0.7 10.7 %copy-start.2 = (f32[512]{0:T(512)S(1)}, f32[512]{0:T(512)}, u32[]{:S(2)}) copy-start(f32[512]{0:T(512)} %param.7) | copy-start | bytes 6148
  7.0 19.7 %all-to-all-start = ((f16[4,8,5120]{2,1,0:T(8,128)(2,1)}), f16[4,8,5120]{2,1,0:T(8,128)(2,1)S(1)}, u32[]{:S(2)}, u32[]{:S(2)}) async-start(f16[4,8,5120]{2,1,0:T(8,128)(2,1)} %pad_maximum_fusion), calls=%async_computation | async-start | bytes 655360 | tf_op jit(solution)/shard_map/all_to_all | solution.py:59
  11.3 85.5 %collective-permute-start = (f32[2,512]{1,0:T(2,128)S(1)}, f32[2,512]{1,0:T(2,128)S(1)}, u32[]{:S(2)}, u32[]{:S(2)}) collective-permute-start(f32[2,512]{1,0:T(2,128)S(1)} %pad_maximum_fusion.3), channel_id=1, source_target_pairs={{0,128},{128,0},{256,384},{384,256},{1,129},{129,1},{257,385},{385... | collective-permute-start | bytes 12296 | tf_op jit(solution)/shard_map/ppermute | solution.py:32
  18.5 79.8 %collective-permute-start.1 = (bf16[256,4096]{1,0:T(8,128)(2,1)}, bf16[256,4096]{1,0:T(8,128)(2,1)S(1)}, u32[]{:S(2)}, u32[]{:S(2)}) collective-permute-start(bf16[256,4096]{1,0:T(8,128)(2,1)} %constant_dynamic-slice_fusion.3), channel_id=1, source_target_pairs={{0,128},{128,0},{256,384},{384,256},{1,129},{129,1},{257,385},{385... | collective-permute-start | bytes 6291464 | tf_op jit(solution)/shard_map/ppermute | solution.py:33
  26.8 70.2 %copy-start.1 = (bf16[512,4096]{1,0:T(8,128)(2,1)S(1)}, bf16[512,4096]{1,0:T(8,128)(2,1)}, u32[]{:S(2)}) copy-start(bf16[512,4096]{1,0:T(8,128)(2,1)} %param.5) | copy-start | bytes 12582916
  98.2 7.0 %collective-permute-start.2 = (bf16[256,4096]{1,0:T(8,128)(2,1)S(1)}, bf16[256,4096]{1,0:T(8,128)(2,1)S(1)}, u32[]{:S(2)}, u32[]{:S(2)}) collective-permute-start(bf16[256,4096]{1,0:T(8,128)(2,1)S(1)} %collective-permute-done.1), channel_id=1, source_target_pairs={{0,1},{1,0},{2,3},{3,2},{4,5},{5,4},{6,7},{7,6},{8,9},{9,8},{10,11... | collective-permute-start | bytes 6291464 | tf_op jit(solution)/shard_map/ppermute | solution.py:36

commit v3 on v2

--- a/solution.py
+++ b/solution.py
@@ -36,9 +36,9 @@
     far_half = lax.ppermute(near_half, "cand", twin)
 
     mine = lax.dynamic_slice_in_dim(cand_index, my_cand * per_dev, per_dev, 1).reshape(-1)
-    owner = winners // per_row
-    won = jnp.take_along_axis(cand_index, (winners % per_row)[:, None], axis=1)[:, 0]
-    won = jnp.where(owner == lax.axis_index(PTS), won, -1)
+    slot = lax.broadcasted_iota(jnp.int32, cand_index.shape, 1)
+    column_of = slot + lax.axis_index(PTS) * per_row
+    won = jnp.sum(jnp.where(column_of == winners[:, None], cand_index + 1, 0), axis=1) - 1
     wanted = jnp.concatenate([mine, won])
     held = steps * per_dev
     pick = jnp.where(
@@ -47,7 +47,6 @@
     picked = lax.dot_general(
         pick, points, (((1,), (0,)), ((), ())), preferred_element_type=jnp.float32
     ).astype(WIRE)
-    owner_x, owner_z = owner // n_z, owner % n_z
 
     piece = steps * width // per_dev
     wins = picked[held:].reshape(per_dev, piece)
@@ -57,11 +56,11 @@
     ]
     sent = jnp.stack([sent[x % steps] for x in range(n_x)])
     along_x = lax.all_to_all(sent, PTS[0], 0, 0, tiled=True)
-    part = per_dev // steps
     slots = n_x * per_dev
+    wins = jnp.sum(along_x[:, :, width:].astype(jnp.float32), axis=0).astype(WIRE)
     wins = jnp.concatenate(
         [
-            lax.dynamic_slice(along_x, (owner_x[t], t * part, width), (1, part, piece)).reshape(
+            wins[t * (per_dev // steps) : (t + 1) * (per_dev // steps)].reshape(
                 slots // steps, steps * width // slots
             )
             for t in range(steps)
@@ -74,8 +73,9 @@
     part = slots // steps
     chosen = jnp.concatenate(
         [
-            lax.dynamic_slice(
-                along_z, (owner_z[t] * slots + t * part, width), (part, piece)
+            sum(
+                along_z[z * slots + t * part : z * slots + (t + 1) * part, width:].astype(jnp.float32)
+                for z in range(n_z)
             ).reshape(1, width)
             for t in range(steps)
         ]

time: 134 us -> 127 us (0.948)
  between operations: 6.05 us -> 0.91 us
  local copies, waits for them, and re-layouts: 6.97 us -> 5.05 us
where the time goes in v3:
time: 127 us
  blocking collectives  95.8 us (75%)
  starting transfers between devices  12.1 us (10%)
  matrix products  10.4 us (8%)
  local copies, waits for them, and re-layouts  5.05 us (4%)
  other arithmetic  2.62 us (2%)
    all_gather x1, blocking collectives, body(): along_z = lax.all_gather(column, PTS[1], axis=0, tiled=True)  70 us
    all_to_all x1, blocking collectives, body(): part = lax.all_to_all(part, PTS, 0, 0, tiled=True)  25.7 us
    dot_general x6, matrix products, dot(): lax.dot_general(a, b, (((1,), (1,)), ((), ())), preferred_element_type=jn...  7.55 us
    all_to_all x1, starting transfers between devices, body(): along_x = lax.all_to_all(sent, PTS[0], 0, 0, tiled=True)  4.29 us
    ppermute x1, starting transfers between devices, body(): there = lax.ppermute(jnp.stack([weights, coverage]), PTS[0], beside)  3.93 us
    dynamic_slice x1, local copies, waits for them, and re-layouts, body(): lax.dynamic_slice_in_dim(points, my_core * half, half, 0)  3.17 us
    dot_general x1, matrix products, body(): lax.dot_general(pick, points, (((1,), (0,)), ((), ())), preferred_element...  2.89 us
  transfers between devices with their start and end apart: 4, of which 0 were waited for; matrix products, arithmetic and copies ran while one was open for 8% of the time, Pallas kernels for 0%

profile of v3, /device:TPU:24, one launch (start us, length us, event | category | flops | bytes accessed | tf_op | source)
XLA Modules:
  0.0 126.9 jit_solution(15586570044977786789)
XLA Ops:
  0.6 0.0 copy-start.2
  0.6 0.0 copy-start.1
  0.7 0.8 constant_dynamic-slice_fusion.5
  1.4 0.1 reshape.78
  1.5 0.9 fusion.65
  2.4 0.1 pad_add_fusion
  2.4 2.9 %convolution_convert_fusion = f16[18,4096]{1,0:T(8,128)(2,1)S(1)} fusion(bf16[512,4096]{1,0:T(8,128)(2,1)} %param.5, s32[18]{0:T(128)S(1)} %pad_add_fusion), kind=kOutput, calls=%fused_computation | convolution fusion | flops 75598848 | bytes 4341832 | tf_op jit(solution)/shard_map/dot_general | solution.py:47
  5.5 0.9 pad_maximum_fusion
  6.3 4.3 %all-to-all-start = ((f16[4,8,5120]{2,1,0:T(8,128)(2,1)}), f16[4,8,5120]{2,1,0:T(8,128)(2,1)S(1)}, u32[]{:S(2)}, u32[]{:S(2)}) async-start(f16[4,8,5120]{2,1,0:T(8,128)(2,1)} %pad_maximum_fusion), calls=%async_computation | async-start | bytes 655360 | tf_op jit(solution)/shard_map/all_to_all | solution.py:58
  10.6 0.0 copy-done.2
  10.6 3.9 %collective-permute-start = (f32[2,512]{1,0:T(2,128)S(1)}, f32[2,512]{1,0:T(2,128)S(1)}, u32[]{:S(2)}, u32[]{:S(2)}) collective-permute-start(f32[2,512]{1,0:T(2,128)S(1)} %pad_maximum_fusion.3), channel_id=1, source_target_pairs={{0,128},{128,0},{256,384},{384,256},{1,129},{129,1},{257,385},{385... | collective-permute-start | bytes 12296 | tf_op jit(solution)/shard_map/ppermute | solution.py:32
  14.6 3.2 %constant_dynamic-slice_fusion.3 = bf16[256,4096]{1,0:T(8,128)(2,1)} fusion(bf16[512,4096]{1,0:T(8,128)(2,1)} %param.5, s32[]{:T(128)S(6)} %select_n.62), kind=kLoop, calls=%fused_computation.58 | loop fusion | bytes 4194308 | tf_op jit(solution)/shard_map/dynamic_slice | solution.py:34
  17.8 1.9 %collective-permute-start.1 = (bf16[256,4096]{1,0:T(8,128)(2,1)}, bf16[256,4096]{1,0:T(8,128)(2,1)S(1)}, u32[]{:S(2)}, u32[]{:S(2)}) collective-permute-start(bf16[256,4096]{1,0:T(8,128)(2,1)} %constant_dynamic-slice_fusion.3), channel_id=1, source_target_pairs={{0,128},{128,0},{256,384},{384,256},{1,129},{129,1},{257,385},{385... | collective-permute-start | bytes 6291464 | tf_op jit(solution)/shard_map/ppermute | solution.py:33
  19.7 0.0 all-to-all-done
  19.8 0.0 copy-start
  19.9 0.1 maximum_maximum_fusion
  19.9 70.0 %all-gather.1 = f16[512,4352]{1,0:T(8,128)(2,1)S(1)} all-gather(f16[32,4352]{1,0:T(8,128)(2,1)S(1)} %maximum_maximum_fusion), channel_id=1, replica_groups=mesh['pts_0'=4,'pts_1'=16,'cand'=8] {'pts_1'}, dimensions={0}, use_global_device_ids=true | all-gather | bytes 4734976 | tf_op jit(solution)/shard_map/all_gather | solution.py:70
  90.0 0.0 collective-permute-done
  90.1 1.2 fusion.54
  91.3 0.0 collective-permute-done.1
  91.3 1.9 %collective-permute-start.2 = (bf16[256,4096]{1,0:T(8,128)(2,1)S(1)}, bf16[256,4096]{1,0:T(8,128)(2,1)S(1)}, u32[]{:S(2)}, u32[]{:S(2)}) collective-permute-start(bf16[256,4096]{1,0:T(8,128)(2,1)S(1)} %collective-permute-done.1), channel_id=1, source_target_pairs={{0,1},{1,0},{2,3},{3,2},{4,5},{5,4},{6,7},{7,6},{8,9},{9,8},{10,11... | collective-permute-start | bytes 6291464 | tf_op jit(solution)/shard_map/ppermute | solution.py:36
  93.3 0.6 maximum_maximum_fusion.1
  93.9 2.4 %fusion.21 = f32[512]{0:T(512)S(1)} fusion(bf16[512,4096]{1,0:T(8,128)(2,1)S(1)} %copy-done, f16[512,4352]{1,0:T(8,128)(2,1)S(1)} %all-gather.1, f32[512]{0:T(512)S(1)} %get-tuple-element.15, f32[512]{0:T(512)S(1)} %copy-done.2), kind=kOutput, calls=%fused_computation.14 | convolution fusion | flops 2150891008 | bytes 8394752 | tf_op jit(solution)/shard_map/dot_general | solution.py:14
  96.3 0.6 fusion.73
  96.9 1.3 %fusion.48 = f32[512]{0:T(512)S(1)} fusion(bf16[256,4096]{1,0:T(8,128)(2,1)S(1)} %collective-permute-done.1, f16[512,4352]{1,0:T(8,128)(2,1)S(1)} %all-gather.1, f32[256]{0:T(256)S(1)} %maximum_select_fusion.2, f32[256]{0:T(256)S(1)} %bitcast.58), kind=kOutput, calls=%fused_computation.23 | convolution fusion | flops 1076493824 | bytes 6295552 | tf_op jit(solution)/shard_map/dot_general | solution.py:14
  98.3 0.0 collective-permute-done.2
  98.3 0.6 fusion.74
  98.9 1.3 %fusion.51 = f32[512]{0:T(512)S(1)} fusion(bf16[256,4096]{1,0:T(8,128)(2,1)S(1)} %collective-permute-done.2, f16[512,4352]{1,0:T(8,128)(2,1)S(1)} %all-gather.1, f32[256]{0:T(256)S(1)} %maximum_select_fusion.1, f32[256]{0:T(256)S(1)} %bitcast.57), kind=kOutput, calls=%fused_computation.24 | convolution fusion | flops 1076493824 | bytes 6295552 | tf_op jit(solution)/shard_map/dot_general | solution.py:14
  100.3 0.1 add.180
  100.4 25.7 %all_to_all.14 = f32[64,1,8]{2,1,0:T(1,128)S(1)} all-to-all(f32[64,1,8]{2,1,0:T(1,128)S(1)} %bitcast.47), channel_id=1, replica_groups=mesh['pts_0'=4,'pts_1'=16,'cand'=8] {'pts_0','pts_1'}, dimensions={0} | all-to-all | bytes 4096 | tf_op jit(solution)/shard_map/all_to_all | solution.py:104
  126.1 0.1 copy.14
  126.2 0.6 copy.11
  (28 shorter events, 0.4 us)
Async XLA Ops:
  0.6 10.0 %copy-start.2 = (f32[512]{0:T(512)S(1)}, f32[512]{0:T(512)}, u32[]{:S(2)}) copy-start(f32[512]{0:T(512)} %param.6) | copy-start | bytes 6148
  0.6 10.0 %copy-start.1 = (f32[512]{0:T(512)S(1)}, f32[512]{0:T(512)}, u32[]{:S(2)}) copy-start(f32[512]{0:T(512)} %param.7) | copy-start | bytes 6148
  6.3 13.4 %all-to-all-start = ((f16[4,8,5120]{2,1,0:T(8,128)(2,1)}), f16[4,8,5120]{2,1,0:T(8,128)(2,1)S(1)}, u32[]{:S(2)}, u32[]{:S(2)}) async-start(f16[4,8,5120]{2,1,0:T(8,128)(2,1)} %pad_maximum_fusion), calls=%async_computation | async-start | bytes 655360 | tf_op jit(solution)/shard_map/all_to_all | solution.py:58
  10.6 79.4 %collective-permute-start = (f32[2,512]{1,0:T(2,128)S(1)}, f32[2,512]{1,0:T(2,128)S(1)}, u32[]{:S(2)}, u32[]{:S(2)}) collective-permute-start(f32[2,512]{1,0:T(2,128)S(1)} %pad_maximum_fusion.3), channel_id=1, source_target_pairs={{0,128},{128,0},{256,384},{384,256},{1,129},{129,1},{257,385},{385... | collective-permute-start | bytes 12296 | tf_op jit(solution)/shard_map/ppermute | solution.py:32
  17.8 73.5 %collective-permute-start.1 = (bf16[256,4096]{1,0:T(8,128)(2,1)}, bf16[256,4096]{1,0:T(8,128)(2,1)S(1)}, u32[]{:S(2)}, u32[]{:S(2)}) collective-permute-start(bf16[256,4096]{1,0:T(8,128)(2,1)} %constant_dynamic-slice_fusion.3), channel_id=1, source_target_pairs={{0,128},{128,0},{256,384},{384,256},{1,129},{129,1},{257,385},{385... | collective-permute-start | bytes 6291464 | tf_op jit(solution)/shard_map/ppermute | solution.py:33
  19.8 70.3 %copy-start = (bf16[512,4096]{1,0:T(8,128)(2,1)S(1)}, bf16[512,4096]{1,0:T(8,128)(2,1)}, u32[]{:S(2)}) copy-start(bf16[512,4096]{1,0:T(8,128)(2,1)} %param.5) | copy-start | bytes 12582916
  91.3 7.0 %collective-permute-start.2 = (bf16[256,4096]{1,0:T(8,128)(2,1)S(1)}, bf16[256,4096]{1,0:T(8,128)(2,1)S(1)}, u32[]{:S(2)}, u32[]{:S(2)}) collective-permute-start(bf16[256,4096]{1,0:T(8,128)(2,1)S(1)} %collective-permute-done.1), channel_id=1, source_target_pairs={{0,1},{1,0},{2,3},{3,2},{4,5},{5,4},{6,7},{7,6},{8,9},{9,8},{10,11... | collective-permute-start | bytes 6291464 | tf_op jit(solution)/shard_map/ppermute | solution.py:36

commit v4 on v3

--- a/solution.py
+++ b/solution.py
@@ -1,6 +1,8 @@
 import jax
 import jax.numpy as jnp
 from jax import lax
+from jax.experimental import pallas as pl
+from jax.experimental.pallas import tpu as pltpu
 from jax.sharding import Mesh
 from jax.sharding import PartitionSpec as P
 
@@ -8,10 +10,90 @@
 PTS_CAND = ("pts_0", "pts_1", "cand")
 WIRE = jnp.float16
 LIFT = 2.0**13
+SUBLANES = 8
 
 
 def dot(a, b):
     return lax.dot_general(a, b, (((1,), (1,)), ((), ())), preferred_element_type=jnp.float32)
+
+
+def fetch(points, cand_index, winners):
+    rows_dev, width = points.shape
+    half = rows_dev // 2
+    steps, per_row = cand_index.shape
+    n_x = lax.axis_size(PTS[0])
+    per_dev = per_row // lax.axis_size("cand")
+    held = steps * per_dev
+    parts = per_dev // steps
+    piece = width // parts
+
+    def kernel(index_ref, winners_ref, points_ref, out_ref, half_ref, *scratch):
+        tiles_ref, rows_ref, wins_ref, stage_ref, sems, half_sems = scratch
+        at = pl.multiple_of(lax.axis_index("cand") % 2 * half, SUBLANES)
+        half_in = pltpu.make_async_copy(
+            points_ref.at[pl.ds(at, half)], stage_ref, half_sems.at[0]
+        )
+        half_out = pltpu.make_async_copy(stage_ref, half_ref, half_sems.at[1])
+        first = lax.axis_index("cand") * per_dev
+        here = lax.axis_index(PTS) * per_row
+        within, copies = [], []
+        for r in range(held + steps):
+            if r < held:
+                row = index_ref[r // per_dev, first + r % per_dev]
+                within.append(row % SUBLANES)
+            else:
+                slot = winners_ref[r - held] - here
+                owned = (slot >= 0) & (slot < per_row)
+                row = index_ref[r - held, jnp.clip(slot, 0, per_row - 1)]
+                within.append(jnp.where(owned, row % SUBLANES, -1))
+            at = pl.multiple_of(row // SUBLANES * SUBLANES, SUBLANES)
+            copies.append(
+                pltpu.make_async_copy(
+                    points_ref.at[pl.ds(at, SUBLANES)], tiles_ref.at[r], sems.at[r]
+                )
+            )
+            copies[-1].start()
+        half_in.start()
+        sublane = lax.broadcasted_iota(jnp.int32, (SUBLANES, width), 0)
+        for r in range(held + steps):
+            if r == per_dev:
+                half_in.wait()
+                half_out.start()
+            copies[r].wait()
+            tile = tiles_ref[r].astype(jnp.float32)
+            row = jnp.sum(jnp.where(sublane == within[r], tile, 0.0), axis=0, keepdims=True)
+            if r < held:
+                rows_ref[r : r + 1] = row
+            else:
+                for k in range(parts):
+                    at = (r - held) * parts + k
+                    wins_ref[at : at + 1] = row[:, k * piece : (k + 1) * piece]
+        for x in range(n_x):
+            rows = rows_ref[x % steps * per_dev : (x % steps + 1) * per_dev]
+            out_ref[x, :, :width] = rows.astype(out_ref.dtype)
+            out_ref[x, :, width:] = wins_ref[...].astype(out_ref.dtype)
+        half_out.wait()
+
+    smem, vmem, hbm = (
+        pl.BlockSpec(memory_space=space) for space in (pltpu.SMEM, pltpu.VMEM, pl.ANY)
+    )
+    return pl.pallas_call(
+        kernel,
+        out_shape=[
+            jax.ShapeDtypeStruct((n_x, per_dev, width + piece), points.dtype),
+            jax.ShapeDtypeStruct((half, width), points.dtype),
+        ],
+        in_specs=[smem, smem, hbm],
+        out_specs=[vmem, hbm],
+        scratch_shapes=[
+            pltpu.VMEM((held + steps, SUBLANES, width), points.dtype),
+            pltpu.VMEM((held, width), jnp.float32),
+            pltpu.VMEM((per_dev, piece), jnp.float32),
+            pltpu.VMEM((half, width), points.dtype),
+            pltpu.SemaphoreType.DMA((held + steps,)),
+            pltpu.SemaphoreType.DMA((2,)),
+        ],
+    )(cand_index, winners, points)
 
 
 def body(points, weights, coverage, cand_index, winners):
@@ -30,31 +112,11 @@
     beside = [(x, x ^ 1) for x in range(n_x)]
     twin = [(c, c ^ 1) for c in range(n_cand)]
     there = lax.ppermute(jnp.stack([weights, coverage]), PTS[0], beside)
-    near_half = lax.ppermute(
-        lax.dynamic_slice_in_dim(points, my_core * half, half, 0), PTS[0], beside
-    )
+    rows, own_half = fetch(points, cand_index, winners)
+    near_half = lax.ppermute(own_half, PTS[0], beside)
     far_half = lax.ppermute(near_half, "cand", twin)
 
-    mine = lax.dynamic_slice_in_dim(cand_index, my_cand * per_dev, per_dev, 1).reshape(-1)
-    slot = lax.broadcasted_iota(jnp.int32, cand_index.shape, 1)
-    column_of = slot + lax.axis_index(PTS) * per_row
-    won = jnp.sum(jnp.where(column_of == winners[:, None], cand_index + 1, 0), axis=1) - 1
-    wanted = jnp.concatenate([mine, won])
-    held = steps * per_dev
-    pick = jnp.where(
-        wanted[:, None] == lax.broadcasted_iota(jnp.int32, (held + steps, rows_dev), 1), LIFT, 0.0
-    ).astype(points.dtype)
-    picked = lax.dot_general(
-        pick, points, (((1,), (0,)), ((), ())), preferred_element_type=jnp.float32
-    ).astype(WIRE)
-
-    piece = steps * width // per_dev
-    wins = picked[held:].reshape(per_dev, piece)
-    sent = [
-        jnp.concatenate([picked[t * per_dev : (t + 1) * per_dev], wins], axis=1)
-        for t in range(steps)
-    ]
-    sent = jnp.stack([sent[x % steps] for x in range(n_x)])
+    sent = (rows.astype(jnp.float32) * LIFT).astype(WIRE)
     along_x = lax.all_to_all(sent, PTS[0], 0, 0, tiled=True)
     slots = n_x * per_dev
     wins = jnp.sum(along_x[:, :, width:].astype(jnp.float32), axis=0).astype(WIRE)

time: 127 us -> 126 us (level)
  Pallas kernels: 0 us -> 5.23 us
  local copies, waits for them, and re-layouts: 5.05 us -> 0.98 us
  matrix products: 10.4 us -> 7.64 us
  blocking collectives: 95.8 us -> 94.3 us
  waiting for transfers between devices: 0.01 us -> 1.51 us
    pallas_call x0 -> x1, Pallas kernels: none -> 5.23 us  [fetch(): pl.pallas_call(kernel, out_shape=[jax.ShapeDtypeStruct((n_x, per_dev, wid...]
    dynamic_slice x2 -> x0, local copies, waits for them, and re-layouts: 3.92 us -> none  [the longest x1 3.17 us: body(): lax.dynamic_slice_in_dim(points, my_core * half, half, 0)]
    dot_general x1 -> x0, matrix products: 2.89 us -> none  [body(): lax.dot_general(pick, points, (((1,), (0,)), ((), ())), preferred_element...]
    convert_element_type x0 -> x1, other arithmetic: none -> 1.78 us  [body(): sent = (rows.astype(jnp.float32) * LIFT).astype(WIRE)]
    all_to_all x1, blocking collectives: 25.7 us -> 24.1 us  [body(): part = lax.all_to_all(part, PTS, 0, 0, tiled=True)]
    all_to_all x1, waiting for transfers between devices: 0.01 us -> 1.5 us  [body(): along_x = lax.all_to_all(sent, PTS[0], 0, 0, tiled=True)]
  transfers between devices with their start and end apart: 4 -> 4, of which waited for: 0 -> 1; matrix products, arithmetic and copies ran while one was open for 8% -> 5% of each run, Pallas kernels for 0% -> 0%
where the time goes in v4:
time: 126 us; the launch traced here: 125 us
  blocking collectives  94.3 us (75%)
  starting transfers between devices  12.1 us (10%)
  matrix products  7.64 us (6%)
  Pallas kernels  5.23 us (4%)
  other arithmetic  2.56 us (2%)
  waiting for transfers between devices  1.51 us (1%)
    all_gather x1, blocking collectives, body(): along_z = lax.all_gather(column, PTS[1], axis=0, tiled=True)  70.2 us
    all_to_all x1, blocking collectives, body(): part = lax.all_to_all(part, PTS, 0, 0, tiled=True)  24.1 us
    dot_general x6, matrix products, dot(): lax.dot_general(a, b, (((1,), (1,)), ((), ())), preferred_element_type=jn...  7.64 us
    pallas_call x1, Pallas kernels, fetch(): pl.pallas_call(kernel, out_shape=[jax.ShapeDtypeStruct((n_x, per_dev, wid...  5.23 us
    all_to_all x1, starting transfers between devices, body(): along_x = lax.all_to_all(sent, PTS[0], 0, 0, tiled=True)  4.29 us
    ppermute x1, starting transfers between devices, body(): there = lax.ppermute(jnp.stack([weights, coverage]), PTS[0], beside)  3.93 us
  transfers between devices with their start and end apart: 4, of which 1 were waited for; matrix products, arithmetic and copies ran while one was open for 5% of the time, Pallas kernels for 0%

profile of v4, /device:TPU:24, one launch (start us, length us, event | category | flops | bytes accessed | tf_op | source)
XLA Modules:
  0.0 125.1 jit_solution(10563743675187820000)
XLA Ops:
  0.6 0.0 copy-start.2
  0.6 0.0 copy-start.1
  0.7 5.2 %shard_map.68 = (bf16[4,8,5120]{2,1,0:T(8,128)(2,1)}, bf16[256,4096]{1,0:T(8,128)(2,1)}) custom-call(s32[2,64]{1,0:T(2,128)} %index_ref.1, s32[2]{0:T(128)} %winners_ref.1, bf16[512,4096]{1,0:T(8,128)(2,1)} %points_ref.1), custom_call_target="tpu_custom_call" | custom-call | tf_op jit(solution)/shard_map/pallas_call | solution.py:80
  5.9 1.8 %multiply_convert_fusion = f16[4,8,5120]{2,1,0:T(8,128)(2,1)} fusion(bf16[4,8,5120]{2,1,0:T(8,128)(2,1)} %get-tuple-element.6), kind=kLoop, calls=%fused_computation.26 | loop fusion | flops 491520 | bytes 655360 | tf_op jit(solution)/shard_map/convert_element_type | solution.py:119
  7.7 4.3 %all-to-all-start = ((f16[4,8,5120]{2,1,0:T(8,128)(2,1)}), f16[4,8,5120]{2,1,0:T(8,128)(2,1)S(1)}, u32[]{:S(2)}, u32[]{:S(2)}) async-start(f16[4,8,5120]{2,1,0:T(8,128)(2,1)} %multiply_convert_fusion), calls=%async_computation | async-start | bytes 655360 | tf_op jit(solution)/shard_map/all_to_all | solution.py:120
  12.0 0.0 copy-done.2
  12.0 0.0 copy-done.1
  12.0 3.9 %collective-permute-start = (f32[2,512]{1,0:T(2,128)S(1)}, f32[2,512]{1,0:T(2,128)S(1)}, u32[]{:S(2)}, u32[]{:S(2)}) collective-permute-start(f32[2,512]{1,0:T(2,128)S(1)} %pad_maximum_fusion), channel_id=1, source_target_pairs={{0,128},{128,0},{256,384},{384,256},{1,129},{129,1},{257,385},{385... | collective-permute-start | bytes 12296 | tf_op jit(solution)/shard_map/ppermute | solution.py:114
  15.9 1.9 %collective-permute-start.1 = (bf16[256,4096]{1,0:T(8,128)(2,1)}, bf16[256,4096]{1,0:T(8,128)(2,1)S(1)}, u32[]{:S(2)}, u32[]{:S(2)}) collective-permute-start(bf16[256,4096]{1,0:T(8,128)(2,1)} %get-tuple-element.9), channel_id=1, source_target_pairs={{0,128},{128,0},{256,384},{384,256},{1,129},{129,1},{257,385},{385... | collective-permute-start | bytes 6291464 | tf_op jit(solution)/shard_map/ppermute | solution.py:116
  17.9 1.5 %all-to-all-done = f16[4,8,5120]{2,1,0:T(8,128)(2,1)S(1)} async-done(((f16[4,8,5120]{2,1,0:T(8,128)(2,1)}), f16[4,8,5120]{2,1,0:T(8,128)(2,1)S(1)}, u32[]{:S(2)}, u32[]{:S(2)}) %all-to-all-start) | async-done | bytes 327712 | tf_op jit(solution)/shard_map/all_to_all | solution.py:120
  19.5 0.0 copy-start
  19.5 0.1 maximum_maximum_fusion
  19.6 70.2 %all-gather.1 = f16[512,4352]{1,0:T(8,128)(2,1)S(1)} all-gather(f16[32,4352]{1,0:T(8,128)(2,1)S(1)} %maximum_maximum_fusion), channel_id=1, replica_groups=mesh['pts_0'=4,'pts_1'=16,'cand'=8] {'pts_1'}, dimensions={0}, use_global_device_ids=true | all-gather | bytes 4734976 | tf_op jit(solution)/shard_map/all_gather | solution.py:132
  89.8 0.0 collective-permute-done
  89.9 0.0 copy-done
  89.9 1.2 fusion.54
  91.1 0.0 collective-permute-done.1
  91.1 1.9 %collective-permute-start.2 = (bf16[256,4096]{1,0:T(8,128)(2,1)S(1)}, bf16[256,4096]{1,0:T(8,128)(2,1)S(1)}, u32[]{:S(2)}, u32[]{:S(2)}) collective-permute-start(bf16[256,4096]{1,0:T(8,128)(2,1)S(1)} %collective-permute-done.1), channel_id=1, source_target_pairs={{0,1},{1,0},{2,3},{3,2},{4,5},{5,4},{6,7},{7,6},{8,9},{9,8},{10,11... | collective-permute-start | bytes 6291464 | tf_op jit(solution)/shard_map/ppermute | solution.py:117
  93.1 0.6 maximum_maximum_fusion.1
  93.7 2.4 %fusion.21 = f32[512]{0:T(512)S(1)} fusion(bf16[512,4096]{1,0:T(8,128)(2,1)S(1)} %copy-done, f16[512,4352]{1,0:T(8,128)(2,1)S(1)} %all-gather.1, f32[512]{0:T(512)S(1)} %get-tuple-element.15, f32[512]{0:T(512)S(1)} %copy-done.2), kind=kOutput, calls=%fused_computation.13 | convolution fusion | flops 2150891008 | bytes 8394752 | tf_op jit(solution)/shard_map/dot_general | solution.py:17
  96.1 0.6 fusion.64
  96.8 1.4 %fusion.48 = f32[512]{0:T(512)S(1)} fusion(bf16[256,4096]{1,0:T(8,128)(2,1)S(1)} %collective-permute-done.1, f16[512,4352]{1,0:T(8,128)(2,1)S(1)} %all-gather.1, f32[256]{0:T(256)S(1)} %maximum_select_fusion.2, f32[256]{0:T(256)S(1)} %bitcast.53), kind=kOutput, calls=%fused_computation.22 | convolution fusion | flops 1076493824 | bytes 6295552 | tf_op jit(solution)/shard_map/dot_general | solution.py:17
  98.2 0.0 collective-permute-done.2
  98.2 0.6 fusion.65
  98.8 1.3 %fusion.51 = f32[512]{0:T(512)S(1)} fusion(bf16[256,4096]{1,0:T(8,128)(2,1)S(1)} %collective-permute-done.2, f16[512,4352]{1,0:T(8,128)(2,1)S(1)} %all-gather.1, f32[256]{0:T(256)S(1)} %maximum_select_fusion.1, f32[256]{0:T(256)S(1)} %bitcast.52), kind=kOutput, calls=%fused_computation.23 | convolution fusion | flops 1076493824 | bytes 6295552 | tf_op jit(solution)/shard_map/dot_general | solution.py:17
  100.2 0.1 add.153
  100.3 24.1 %all_to_all.14 = f32[64,1,8]{2,1,0:T(1,128)S(1)} all-to-all(f32[64,1,8]{2,1,0:T(1,128)S(1)} %bitcast.42), channel_id=1, replica_groups=mesh['pts_0'=4,'pts_1'=16,'cand'=8] {'pts_0','pts_1'}, dimensions={0} | all-to-all | bytes 4096 | tf_op jit(solution)/shard_map/all_to_all | solution.py:166
  124.4 0.1 copy.14
  124.5 0.6 copy.11
  (20 shorter events, 0.3 us)
Async XLA Ops:
  0.6 11.3 %copy-start.2 = (f32[512]{0:T(512)S(1)}, f32[512]{0:T(512)}, u32[]{:S(2)}) copy-start(f32[512]{0:T(512)} %param.6) | copy-start | bytes 6148
  0.6 11.3 %copy-start.1 = (f32[512]{0:T(512)S(1)}, f32[512]{0:T(512)}, u32[]{:S(2)}) copy-start(f32[512]{0:T(512)} %param.7) | copy-start | bytes 6148
  7.7 11.7 %all-to-all-start = ((f16[4,8,5120]{2,1,0:T(8,128)(2,1)}), f16[4,8,5120]{2,1,0:T(8,128)(2,1)S(1)}, u32[]{:S(2)}, u32[]{:S(2)}) async-start(f16[4,8,5120]{2,1,0:T(8,128)(2,1)} %multiply_convert_fusion), calls=%async_computation | async-start | bytes 655360 | tf_op jit(solution)/shard_map/all_to_all | solution.py:120
  12.0 77.8 %collective-permute-start = (f32[2,512]{1,0:T(2,128)S(1)}, f32[2,512]{1,0:T(2,128)S(1)}, u32[]{:S(2)}, u32[]{:S(2)}) collective-permute-start(f32[2,512]{1,0:T(2,128)S(1)} %pad_maximum_fusion), channel_id=1, source_target_pairs={{0,128},{128,0},{256,384},{384,256},{1,129},{129,1},{257,385},{385... | collective-permute-start | bytes 12296 | tf_op jit(solution)/shard_map/ppermute | solution.py:114
  15.9 75.2 %collective-permute-start.1 = (bf16[256,4096]{1,0:T(8,128)(2,1)}, bf16[256,4096]{1,0:T(8,128)(2,1)S(1)}, u32[]{:S(2)}, u32[]{:S(2)}) collective-permute-start(bf16[256,4096]{1,0:T(8,128)(2,1)} %get-tuple-element.9), channel_id=1, source_target_pairs={{0,128},{128,0},{256,384},{384,256},{1,129},{129,1},{257,385},{385... | collective-permute-start | bytes 6291464 | tf_op jit(solution)/shard_map/ppermute | solution.py:116
  19.5 70.5 %copy-start = (bf16[512,4096]{1,0:T(8,128)(2,1)S(1)}, bf16[512,4096]{1,0:T(8,128)(2,1)}, u32[]{:S(2)}) copy-start(bf16[512,4096]{1,0:T(8,128)(2,1)} %points_ref.1) | copy-start | bytes 12582916
  91.1 7.0 %collective-permute-start.2 = (bf16[256,4096]{1,0:T(8,128)(2,1)S(1)}, bf16[256,4096]{1,0:T(8,128)(2,1)S(1)}, u32[]{:S(2)}, u32[]{:S(2)}) collective-permute-start(bf16[256,4096]{1,0:T(8,128)(2,1)S(1)} %collective-permute-done.1), channel_id=1, source_target_pairs={{0,1},{1,0},{2,3},{3,2},{4,5},{5,4},{6,7},{7,6},{8,9},{9,8},{10,11... | collective-permute-start | bytes 6291464 | tf_op jit(solution)/shard_map/ppermute | solution.py:117

commit v5 on v4

--- a/solution.py
+++ b/solution.py
@@ -93,6 +93,7 @@
             pltpu.SemaphoreType.DMA((held + steps,)),
             pltpu.SemaphoreType.DMA((2,)),
         ],
+        compiler_params=pltpu.CompilerParams(vmem_limit_bytes=52 * 1024 * 1024),
     )(cand_index, winners, points)
 
 

time: 126 us -> 125 us (level)
  local copies, waits for them, and re-layouts: 0.98 us -> 2.31 us
    unnamed x10 -> x14, local copies, waits for them, and re-layouts: 0.77 us -> 2.09 us
where the time goes in v5:
time: 125 us; the launch traced here: 124 us
  blocking collectives  94.3 us (75%)
  starting transfers between devices  12.1 us (10%)
  matrix products  7.64 us (6%)
  Pallas kernels  4.19 us (3%)
  local copies, waits for them, and re-layouts  2.31 us (2%)
  other arithmetic  1.61 us (1%)
  waiting for transfers between devices  1.51 us (1%)
    all_gather x1, blocking collectives, body(): along_z = lax.all_gather(column, PTS[1], axis=0, tiled=True)  70.2 us
    all_to_all x1, blocking collectives, body(): part = lax.all_to_all(part, PTS, 0, 0, tiled=True)  24.1 us
    dot_general x6, matrix products, dot(): lax.dot_general(a, b, (((1,), (1,)), ((), ())), preferred_element_type=jn...  7.64 us
    all_to_all x1, starting transfers between devices, body(): along_x = lax.all_to_all(sent, PTS[0], 0, 0, tiled=True)  4.29 us
    pallas_call x1, Pallas kernels, fetch(): pl.pallas_call(kernel, out_shape=[jax.ShapeDtypeStruct((n_x, per_dev, wid...  4.19 us
    ppermute x1, starting transfers between devices, body(): there = lax.ppermute(jnp.stack([weights, coverage]), PTS[0], beside)  3.93 us
  transfers between devices with their start and end apart: 4, of which 1 were waited for; matrix products, arithmetic and copies ran while one was open for 5% of the time, Pallas kernels for 0%

profile of v5, /device:TPU:24, one launch (start us, length us, event | category | flops | bytes accessed | tf_op | source)
XLA Modules:
  0.0 124.5 jit_solution(31699278315193565)
XLA Ops:
  0.6 0.0 copy-start
  0.6 0.7 copy-done
  1.3 0.0 copy-start.1
  1.3 0.7 copy-done.1
  2.0 0.0 copy-start.3
  2.0 4.2 %shard_map.68 = (bf16[4,8,5120]{2,1,0:T(8,128)(2,1)S(1)}, bf16[256,4096]{1,0:T(8,128)(2,1)}) custom-call(s32[2,64]{1,0:T(2,128)S(1)} %copy-done, s32[2]{0:T(128)S(1)} %copy-done.1, bf16[512,4096]{1,0:T(8,128)(2,1)} %points_ref.1), custom_call_target="tpu_custom_call" | custom-call | tf_op jit(solution)/shard_map/pallas_call | solution.py:80
  6.2 0.8 multiply_convert_fusion
  7.0 4.3 %all-to-all-start = ((f16[4,8,5120]{2,1,0:T(8,128)(2,1)}), f16[4,8,5120]{2,1,0:T(8,128)(2,1)S(1)}, u32[]{:S(2)}, u32[]{:S(2)}) async-start(f16[4,8,5120]{2,1,0:T(8,128)(2,1)} %multiply_convert_fusion), calls=%async_computation | async-start | bytes 655360 | tf_op jit(solution)/shard_map/all_to_all | solution.py:121
  11.3 0.0 copy-done.3
  11.3 0.0 copy-done.4
  11.3 3.9 %collective-permute-start = (f32[2,512]{1,0:T(2,128)S(1)}, f32[2,512]{1,0:T(2,128)S(1)}, u32[]{:S(2)}, u32[]{:S(2)}) collective-permute-start(f32[2,512]{1,0:T(2,128)S(1)} %pad_maximum_fusion), channel_id=1, source_target_pairs={{0,128},{128,0},{256,384},{384,256},{1,129},{129,1},{257,385},{385... | collective-permute-start | bytes 12296 | tf_op jit(solution)/shard_map/ppermute | solution.py:115
  15.2 1.9 %collective-permute-start.1 = (bf16[256,4096]{1,0:T(8,128)(2,1)}, bf16[256,4096]{1,0:T(8,128)(2,1)S(1)}, u32[]{:S(2)}, u32[]{:S(2)}) collective-permute-start(bf16[256,4096]{1,0:T(8,128)(2,1)} %get-tuple-element.9), channel_id=1, source_target_pairs={{0,128},{128,0},{256,384},{384,256},{1,129},{129,1},{257,385},{385... | collective-permute-start | bytes 6291464 | tf_op jit(solution)/shard_map/ppermute | solution.py:117
  17.2 1.5 %all-to-all-done = f16[4,8,5120]{2,1,0:T(8,128)(2,1)S(1)} async-done(((f16[4,8,5120]{2,1,0:T(8,128)(2,1)}), f16[4,8,5120]{2,1,0:T(8,128)(2,1)S(1)}, u32[]{:S(2)}, u32[]{:S(2)}) %all-to-all-start) | async-done | bytes 327712 | tf_op jit(solution)/shard_map/all_to_all | solution.py:121
  18.8 0.0 copy-start.2
  18.9 0.1 maximum_maximum_fusion
  18.9 70.2 %all-gather.1 = f16[512,4352]{1,0:T(8,128)(2,1)S(1)} all-gather(f16[32,4352]{1,0:T(8,128)(2,1)S(1)} %maximum_maximum_fusion), channel_id=1, replica_groups=mesh['pts_0'=4,'pts_1'=16,'cand'=8] {'pts_1'}, dimensions={0}, use_global_device_ids=true | all-gather | bytes 4734976 | tf_op jit(solution)/shard_map/all_gather | solution.py:133
  89.1 0.0 collective-permute-done
  89.3 0.0 copy-done.2
  89.3 1.2 fusion.54
  90.5 0.0 collective-permute-done.1
  90.5 1.9 %collective-permute-start.2 = (bf16[256,4096]{1,0:T(8,128)(2,1)S(1)}, bf16[256,4096]{1,0:T(8,128)(2,1)S(1)}, u32[]{:S(2)}, u32[]{:S(2)}) collective-permute-start(bf16[256,4096]{1,0:T(8,128)(2,1)S(1)} %collective-permute-done.1), channel_id=1, source_target_pairs={{0,1},{1,0},{2,3},{3,2},{4,5},{5,4},{6,7},{7,6},{8,9},{9,8},{10,11... | collective-permute-start | bytes 6291464 | tf_op jit(solution)/shard_map/ppermute | solution.py:118
  92.4 0.6 maximum_maximum_fusion.1
  93.0 2.4 %fusion.21 = f32[512]{0:T(512)S(1)} fusion(bf16[512,4096]{1,0:T(8,128)(2,1)S(1)} %copy-done.2, f16[512,4352]{1,0:T(8,128)(2,1)S(1)} %all-gather.1, f32[512]{0:T(512)S(1)} %get-tuple-element.15, f32[512]{0:T(512)S(1)} %copy-done.4), kind=kOutput, calls=%fused_computation.13 | convolution fusion | flops 2150891008 | bytes 8394752 | tf_op jit(solution)/shard_map/dot_general | solution.py:17
  95.4 0.6 fusion.64
  96.1 1.4 %fusion.48 = f32[512]{0:T(512)S(1)} fusion(bf16[256,4096]{1,0:T(8,128)(2,1)S(1)} %collective-permute-done.1, f16[512,4352]{1,0:T(8,128)(2,1)S(1)} %all-gather.1, f32[256]{0:T(256)S(1)} %maximum_select_fusion.2, f32[256]{0:T(256)S(1)} %bitcast.53), kind=kOutput, calls=%fused_computation.22 | convolution fusion | flops 1076493824 | bytes 6295552 | tf_op jit(solution)/shard_map/dot_general | solution.py:17
  97.5 0.0 collective-permute-done.2
  97.5 0.6 fusion.65
  98.2 1.3 %fusion.51 = f32[512]{0:T(512)S(1)} fusion(bf16[256,4096]{1,0:T(8,128)(2,1)S(1)} %collective-permute-done.2, f16[512,4352]{1,0:T(8,128)(2,1)S(1)} %all-gather.1, f32[256]{0:T(256)S(1)} %maximum_select_fusion.1, f32[256]{0:T(256)S(1)} %bitcast.52), kind=kOutput, calls=%fused_computation.23 | convolution fusion | flops 1076493824 | bytes 6295552 | tf_op jit(solution)/shard_map/dot_general | solution.py:17
  99.5 0.1 add.153
  99.6 24.1 %all_to_all.14 = f32[64,1,8]{2,1,0:T(1,128)S(1)} all-to-all(f32[64,1,8]{2,1,0:T(1,128)S(1)} %bitcast.42), channel_id=1, replica_groups=mesh['pts_0'=4,'pts_1'=16,'cand'=8] {'pts_0','pts_1'}, dimensions={0} | all-to-all | bytes 4096 | tf_op jit(solution)/shard_map/all_to_all | solution.py:167
  123.7 0.1 copy.14
  123.8 0.6 copy.11
  (21 shorter events, 0.3 us)
Async XLA Ops:
  0.6 0.7 copy-start
  1.3 0.7 copy-start.1
  2.0 9.3 %copy-start.3 = (f32[512]{0:T(512)S(1)}, f32[512]{0:T(512)}, u32[]{:S(2)}) copy-start(f32[512]{0:T(512)} %param.7) | copy-start | bytes 6148
  2.0 9.3 %copy-start.4 = (f32[512]{0:T(512)S(1)}, f32[512]{0:T(512)}, u32[]{:S(2)}) copy-start(f32[512]{0:T(512)} %param.6) | copy-start | bytes 6148
  7.0 11.7 %all-to-all-start = ((f16[4,8,5120]{2,1,0:T(8,128)(2,1)}), f16[4,8,5120]{2,1,0:T(8,128)(2,1)S(1)}, u32[]{:S(2)}, u32[]{:S(2)}) async-start(f16[4,8,5120]{2,1,0:T(8,128)(2,1)} %multiply_convert_fusion), calls=%async_computation | async-start | bytes 655360 | tf_op jit(solution)/shard_map/all_to_all | solution.py:121
  11.3 77.8 %collective-permute-start = (f32[2,512]{1,0:T(2,128)S(1)}, f32[2,512]{1,0:T(2,128)S(1)}, u32[]{:S(2)}, u32[]{:S(2)}) collective-permute-start(f32[2,512]{1,0:T(2,128)S(1)} %pad_maximum_fusion), channel_id=1, source_target_pairs={{0,128},{128,0},{256,384},{384,256},{1,129},{129,1},{257,385},{385... | collective-permute-start | bytes 12296 | tf_op jit(solution)/shard_map/ppermute | solution.py:115
  15.2 75.2 %collective-permute-start.1 = (bf16[256,4096]{1,0:T(8,128)(2,1)}, bf16[256,4096]{1,0:T(8,128)(2,1)S(1)}, u32[]{:S(2)}, u32[]{:S(2)}) collective-permute-start(bf16[256,4096]{1,0:T(8,128)(2,1)} %get-tuple-element.9), channel_id=1, source_target_pairs={{0,128},{128,0},{256,384},{384,256},{1,129},{129,1},{257,385},{385... | collective-permute-start | bytes 6291464 | tf_op jit(solution)/shard_map/ppermute | solution.py:117
  18.8 70.5 %copy-start.2 = (bf16[512,4096]{1,0:T(8,128)(2,1)S(1)}, bf16[512,4096]{1,0:T(8,128)(2,1)}, u32[]{:S(2)}) copy-start(bf16[512,4096]{1,0:T(8,128)(2,1)} %points_ref.1) | copy-start | bytes 12582916
  90.5 7.0 %collective-permute-start.2 = (bf16[256,4096]{1,0:T(8,128)(2,1)S(1)}, bf16[256,4096]{1,0:T(8,128)(2,1)S(1)}, u32[]{:S(2)}, u32[]{:S(2)}) collective-permute-start(bf16[256,4096]{1,0:T(8,128)(2,1)S(1)} %collective-permute-done.1), channel_id=1, source_target_pairs={{0,1},{1,0},{2,3},{3,2},{4,5},{5,4},{6,7},{7,6},{8,9},{9,8},{10,11... | collective-permute-start | bytes 6291464 | tf_op jit(solution)/shard_map/ppermute | solution.py:118

commit v6 on v5

--- a/solution.py
+++ b/solution.py
@@ -34,6 +34,7 @@
             points_ref.at[pl.ds(at, half)], stage_ref, half_sems.at[0]
         )
         half_out = pltpu.make_async_copy(stage_ref, half_ref, half_sems.at[1])
+        half_in.start()
         first = lax.axis_index("cand") * per_dev
         here = lax.axis_index(PTS) * per_row
         within, copies = [], []
@@ -53,7 +54,6 @@
                 )
             )
             copies[-1].start()
-        half_in.start()
         sublane = lax.broadcasted_iota(jnp.int32, (SUBLANES, width), 0)
         for r in range(held + steps):
             if r == per_dev:

time: 125 us -> 125 us (level)
  no operation moved by 1% of the time
where the time goes in v6:
time: 125 us; the launch traced here: 124 us
  blocking collectives  94.3 us (75%)
  starting transfers between devices  12.1 us (10%)
  matrix products  7.64 us (6%)
  Pallas kernels  4.15 us (3%)
  local copies, waits for them, and re-layouts  2.31 us (2%)
  other arithmetic  1.61 us (1%)
  waiting for transfers between devices  1.51 us (1%)
    all_gather x1, blocking collectives, body(): along_z = lax.all_gather(column, PTS[1], axis=0, tiled=True)  70.2 us
    all_to_all x1, blocking collectives, body(): part = lax.all_to_all(part, PTS, 0, 0, tiled=True)  24.1 us
    dot_general x6, matrix products, dot(): lax.dot_general(a, b, (((1,), (1,)), ((), ())), preferred_element_type=jn...  7.64 us
    all_to_all x1, starting transfers between devices, body(): along_x = lax.all_to_all(sent, PTS[0], 0, 0, tiled=True)  4.29 us
    pallas_call x1, Pallas kernels, fetch(): pl.pallas_call(kernel, out_shape=[jax.ShapeDtypeStruct((n_x, per_dev, wid...  4.15 us
    ppermute x1, starting transfers between devices, body(): there = lax.ppermute(jnp.stack([weights, coverage]), PTS[0], beside)  3.93 us
  transfers between devices with their start and end apart: 4, of which 1 were waited for; matrix products, arithmetic and copies ran while one was open for 5% of the time, Pallas kernels for 0%

profile of v6, /device:TPU:24, one launch (start us, length us, event | category | flops | bytes accessed | tf_op | source)
XLA Modules:
  0.0 124.4 jit_solution(15792410576758531671)
XLA Ops:
  0.6 0.0 copy-start
  0.6 0.7 copy-done
  1.3 0.0 copy-start.1
  1.3 0.7 copy-done.1
  2.0 0.0 copy-start.3
  2.0 4.1 %shard_map.68 = (bf16[4,8,5120]{2,1,0:T(8,128)(2,1)S(1)}, bf16[256,4096]{1,0:T(8,128)(2,1)}) custom-call(s32[2,64]{1,0:T(2,128)S(1)} %copy-done, s32[2]{0:T(128)S(1)} %copy-done.1, bf16[512,4096]{1,0:T(8,128)(2,1)} %points_ref.1), custom_call_target="tpu_custom_call" | custom-call | tf_op jit(solution)/shard_map/pallas_call | solution.py:80
  6.1 0.8 multiply_convert_fusion
  7.0 4.3 %all-to-all-start = ((f16[4,8,5120]{2,1,0:T(8,128)(2,1)}), f16[4,8,5120]{2,1,0:T(8,128)(2,1)S(1)}, u32[]{:S(2)}, u32[]{:S(2)}) async-start(f16[4,8,5120]{2,1,0:T(8,128)(2,1)} %multiply_convert_fusion), calls=%async_computation | async-start | bytes 655360 | tf_op jit(solution)/shard_map/all_to_all | solution.py:121
  11.2 0.0 copy-done.3
  11.3 0.0 copy-done.4
  11.3 3.9 %collective-permute-start = (f32[2,512]{1,0:T(2,128)S(1)}, f32[2,512]{1,0:T(2,128)S(1)}, u32[]{:S(2)}, u32[]{:S(2)}) collective-permute-start(f32[2,512]{1,0:T(2,128)S(1)} %pad_maximum_fusion), channel_id=1, source_target_pairs={{0,128},{128,0},{256,384},{384,256},{1,129},{129,1},{257,385},{385... | collective-permute-start | bytes 12296 | tf_op jit(solution)/shard_map/ppermute | solution.py:115
  15.2 1.9 %collective-permute-start.1 = (bf16[256,4096]{1,0:T(8,128)(2,1)}, bf16[256,4096]{1,0:T(8,128)(2,1)S(1)}, u32[]{:S(2)}, u32[]{:S(2)}) collective-permute-start(bf16[256,4096]{1,0:T(8,128)(2,1)} %get-tuple-element.9), channel_id=1, source_target_pairs={{0,128},{128,0},{256,384},{384,256},{1,129},{129,1},{257,385},{385... | collective-permute-start | bytes 6291464 | tf_op jit(solution)/shard_map/ppermute | solution.py:117
  17.2 1.5 %all-to-all-done = f16[4,8,5120]{2,1,0:T(8,128)(2,1)S(1)} async-done(((f16[4,8,5120]{2,1,0:T(8,128)(2,1)}), f16[4,8,5120]{2,1,0:T(8,128)(2,1)S(1)}, u32[]{:S(2)}, u32[]{:S(2)}) %all-to-all-start) | async-done | bytes 327712 | tf_op jit(solution)/shard_map/all_to_all | solution.py:121
  18.8 0.0 copy-start.2
  18.8 0.1 maximum_maximum_fusion
  18.9 70.2 %all-gather.1 = f16[512,4352]{1,0:T(8,128)(2,1)S(1)} all-gather(f16[32,4352]{1,0:T(8,128)(2,1)S(1)} %maximum_maximum_fusion), channel_id=1, replica_groups=mesh['pts_0'=4,'pts_1'=16,'cand'=8] {'pts_1'}, dimensions={0}, use_global_device_ids=true | all-gather | bytes 4734976 | tf_op jit(solution)/shard_map/all_gather | solution.py:133
  89.1 0.0 collective-permute-done
  89.2 0.0 copy-done.2
  89.2 1.2 fusion.54
  90.4 0.0 collective-permute-done.1
  90.4 1.9 %collective-permute-start.2 = (bf16[256,4096]{1,0:T(8,128)(2,1)S(1)}, bf16[256,4096]{1,0:T(8,128)(2,1)S(1)}, u32[]{:S(2)}, u32[]{:S(2)}) collective-permute-start(bf16[256,4096]{1,0:T(8,128)(2,1)S(1)} %collective-permute-done.1), channel_id=1, source_target_pairs={{0,1},{1,0},{2,3},{3,2},{4,5},{5,4},{6,7},{7,6},{8,9},{9,8},{10,11... | collective-permute-start | bytes 6291464 | tf_op jit(solution)/shard_map/ppermute | solution.py:118
  92.4 0.6 maximum_maximum_fusion.1
  93.0 2.4 %fusion.21 = f32[512]{0:T(512)S(1)} fusion(bf16[512,4096]{1,0:T(8,128)(2,1)S(1)} %copy-done.2, f16[512,4352]{1,0:T(8,128)(2,1)S(1)} %all-gather.1, f32[512]{0:T(512)S(1)} %get-tuple-element.15, f32[512]{0:T(512)S(1)} %copy-done.4), kind=kOutput, calls=%fused_computation.13 | convolution fusion | flops 2150891008 | bytes 8394752 | tf_op jit(solution)/shard_map/dot_general | solution.py:17
  95.4 0.6 fusion.64
  96.1 1.4 %fusion.48 = f32[512]{0:T(512)S(1)} fusion(bf16[256,4096]{1,0:T(8,128)(2,1)S(1)} %collective-permute-done.1, f16[512,4352]{1,0:T(8,128)(2,1)S(1)} %all-gather.1, f32[256]{0:T(256)S(1)} %maximum_select_fusion.2, f32[256]{0:T(256)S(1)} %bitcast.53), kind=kOutput, calls=%fused_computation.22 | convolution fusion | flops 1076493824 | bytes 6295552 | tf_op jit(solution)/shard_map/dot_general | solution.py:17
  97.5 0.0 collective-permute-done.2
  97.5 0.6 fusion.65
  98.1 1.3 %fusion.51 = f32[512]{0:T(512)S(1)} fusion(bf16[256,4096]{1,0:T(8,128)(2,1)S(1)} %collective-permute-done.2, f16[512,4352]{1,0:T(8,128)(2,1)S(1)} %all-gather.1, f32[256]{0:T(256)S(1)} %maximum_select_fusion.1, f32[256]{0:T(256)S(1)} %bitcast.52), kind=kOutput, calls=%fused_computation.23 | convolution fusion | flops 1076493824 | bytes 6295552 | tf_op jit(solution)/shard_map/dot_general | solution.py:17
  99.5 0.1 add.153
  99.6 24.1 %all_to_all.14 = f32[64,1,8]{2,1,0:T(1,128)S(1)} all-to-all(f32[64,1,8]{2,1,0:T(1,128)S(1)} %bitcast.42), channel_id=1, replica_groups=mesh['pts_0'=4,'pts_1'=16,'cand'=8] {'pts_0','pts_1'}, dimensions={0} | all-to-all | bytes 4096 | tf_op jit(solution)/shard_map/all_to_all | solution.py:167
  123.7 0.1 copy.14
  123.8 0.6 copy.11
  (21 shorter events, 0.3 us)
Async XLA Ops:
  0.6 0.7 copy-start
  1.3 0.7 copy-start.1
  2.0 9.3 %copy-start.3 = (f32[512]{0:T(512)S(1)}, f32[512]{0:T(512)}, u32[]{:S(2)}) copy-start(f32[512]{0:T(512)} %param.7) | copy-start | bytes 6148
  2.0 9.3 %copy-start.4 = (f32[512]{0:T(512)S(1)}, f32[512]{0:T(512)}, u32[]{:S(2)}) copy-start(f32[512]{0:T(512)} %param.6) | copy-start | bytes 6148
  7.0 11.7 %all-to-all-start = ((f16[4,8,5120]{2,1,0:T(8,128)(2,1)}), f16[4,8,5120]{2,1,0:T(8,128)(2,1)S(1)}, u32[]{:S(2)}, u32[]{:S(2)}) async-start(f16[4,8,5120]{2,1,0:T(8,128)(2,1)} %multiply_convert_fusion), calls=%async_computation | async-start | bytes 655360 | tf_op jit(solution)/shard_map/all_to_all | solution.py:121
  11.3 77.8 %collective-permute-start = (f32[2,512]{1,0:T(2,128)S(1)}, f32[2,512]{1,0:T(2,128)S(1)}, u32[]{:S(2)}, u32[]{:S(2)}) collective-permute-start(f32[2,512]{1,0:T(2,128)S(1)} %pad_maximum_fusion), channel_id=1, source_target_pairs={{0,128},{128,0},{256,384},{384,256},{1,129},{129,1},{257,385},{385... | collective-permute-start | bytes 12296 | tf_op jit(solution)/shard_map/ppermute | solution.py:115
  15.2 75.2 %collective-permute-start.1 = (bf16[256,4096]{1,0:T(8,128)(2,1)}, bf16[256,4096]{1,0:T(8,128)(2,1)S(1)}, u32[]{:S(2)}, u32[]{:S(2)}) collective-permute-start(bf16[256,4096]{1,0:T(8,128)(2,1)} %get-tuple-element.9), channel_id=1, source_target_pairs={{0,128},{128,0},{256,384},{384,256},{1,129},{129,1},{257,385},{385... | collective-permute-start | bytes 6291464 | tf_op jit(solution)/shard_map/ppermute | solution.py:117
  18.8 70.5 %copy-start.2 = (bf16[512,4096]{1,0:T(8,128)(2,1)S(1)}, bf16[512,4096]{1,0:T(8,128)(2,1)}, u32[]{:S(2)}) copy-start(bf16[512,4096]{1,0:T(8,128)(2,1)} %points_ref.1) | copy-start | bytes 12582916
  90.4 7.0 %collective-permute-start.2 = (bf16[256,4096]{1,0:T(8,128)(2,1)S(1)}, bf16[256,4096]{1,0:T(8,128)(2,1)S(1)}, u32[]{:S(2)}, u32[]{:S(2)}) collective-permute-start(bf16[256,4096]{1,0:T(8,128)(2,1)S(1)} %collective-permute-done.1), channel_id=1, source_target_pairs={{0,1},{1,0},{2,3},{3,2},{4,5},{5,4},{6,7},{7,6},{8,9},{9,8},{10,11... | collective-permute-start | bytes 6291464 | tf_op jit(solution)/shard_map/ppermute | solution.py:118
